TPU v7x, 256 devices: a whole 4x4x8 slice. The times are simulated.
256 devices in a mesh: ctx: 8 (over x, core), exp: 32 (over y, z).
Axes of the slice: x: 4, y: 4, z: 8, core: 2. Of those that a mesh axis runs over, the one named last changes fastest.
Arguments:
- queries: bfloat16 [32, 1024, 1024], P('exp', 'ctx'), may hold values from -6 to 6
- keys: bfloat16 [32, 1024, 1024], P('exp', 'ctx'), may hold values from -6 to 6
- values: bfloat16 [32, 1024, 2048], P('exp', 'ctx'), may hold values from -6 to 6
- out_gate: bfloat16 [32, 1024, 2048], P('exp', 'ctx'), may hold values from -6 to 6
- write_rate: float32 [32, 1024, 16], P('exp', 'ctx'), may hold values from 0.02 to 0.2
- decay: float32 [32, 1024, 16], P('exp', 'ctx'), may hold values from 0.6 to 1
- head_gain: float32 [128], replicated, may hold values from 0.1 to 1.9
- residual: bfloat16 [32, 1024, 2048], P('exp', 'ctx'), may hold values from -6 to 6
- out_proj: bfloat16 [2048, 2048], P('ctx'), may hold values from -0.125 to 0.125
- ffn_gain: float32 [2048], replicated, may hold values from 0.25 to 1.75
- expert_ids: int32 [32, 1024, 10], P('exp', 'ctx'), may hold values from 0 to 511, all different within a row; in each aligned block of 128 rows (0 to 127, 128 to 255, ..., all dimensions but the last counted through in order) at most 4 rows name the same one
- route_weight: float32 [32, 1024, 10], P('exp', 'ctx'), may hold values from 0.1 to 0.4
- w_gate: bfloat16 [256, 2048, 512], P(('ctx', 'exp')), may hold values from -0.125 to 0.125
- w_up: bfloat16 [256, 2048, 512], P(('ctx', 'exp')), may hold values from -0.125 to 0.125
- w_down: bfloat16 [256, 512, 2048], P(('ctx', 'exp')), may hold values from -0.25 to 0.25
- ablate_mask: int32 [32, 1024], P('exp', 'ctx'), may hold values 0 or 1
- direction: float32 [2048], replicated, may hold values from -6 to 6
Outputs:
- layer_out: bfloat16 [32, 1024, 2048], P('exp', 'ctx')
Inputs may be any that keep to these rules, and one draw needn't show every extreme that they name: `expert_ids`: A token's 10 experts differ; within the rows of one device (aligned blocks of 128 tokens of a sequence) no expert is named more than 4 times.
All inputs are finite; a program needn't handle non-finite values. No bound on the sum of `ablate_mask` on one device may be relied on, other than what follows from the above.
Results may differ from a plain program's by a relative error of at most 0.0044.
Values may be sent and summed in bfloat16 or wider, within the bound.
A program may use at most 128 MiB of HBM per device.

v0:
```python
import jax
import jax.numpy as jnp
from jax import lax
from jax.sharding import PartitionSpec as P

D = 2048
CONTENT_MIXERS = 16
KH = 8
DK = 128
DV = 128
TOP = 10
CAP = 4


HIGHEST = lax.Precision.HIGHEST


def passed_along(block, axis, distance):
    devices = range(lax.axis_size(axis))
    route = [(i - distance, i) for i in devices if i - distance in devices]
    return lax.ppermute(block, axis, route)


def block_maps(query_f, key_unit, value_f, write_f, decay_f):
    length_b = decay_f.shape[-1]
    width_k = key_unit.shape[-1]
    log_decay = jnp.cumsum(jnp.log(decay_f), axis=-1)
    row_ids = lax.broadcasted_iota(jnp.int32, (length_b, length_b), 0)
    col_ids = lax.broadcasted_iota(jnp.int32, (length_b, length_b), 1)
    on_after = (row_ids >= col_ids).astype(jnp.float32)
    strictly = (row_ids > col_ids).astype(jnp.float32)
    ratios = jnp.exp(jnp.minimum(log_decay[..., :, None] - log_decay[..., None, :], 0.0)) * on_after
    cumulative = jnp.exp(log_decay)
    key_dots = jnp.einsum("...id,...jd->...ij", key_unit, key_unit, precision=HIGHEST)
    system = (
        jnp.eye(length_b, dtype=jnp.float32) + write_f[..., :, None] * ratios * strictly * key_dots
    )
    writes = jax.scipy.linalg.solve_triangular(
        system, write_f[..., None] * value_f, lower=True, unit_diagonal=True
    )
    erases = jax.scipy.linalg.solve_triangular(
        system, (write_f * cumulative)[..., None] * key_unit, lower=True, unit_diagonal=True
    )
    scores = jnp.einsum("...id,...jd->...ij", query_f, key_unit, precision=HIGHEST) * ratios
    local_out = jnp.einsum("...ij,...jv->...iv", scores, writes, precision=HIGHEST)
    query_eff = cumulative[..., None] * query_f - jnp.einsum(
        "...ij,...jd->...id", scores, erases, precision=HIGHEST
    )
    remaining = jnp.exp(log_decay[..., -1:] - log_decay)
    weighted = remaining[..., None] * key_unit
    carried = jnp.einsum("...jd,...je->...de", weighted, erases, precision=HIGHEST)
    transition = (
        cumulative[..., -1][..., None, None] * jnp.eye(width_k, dtype=jnp.float32) - carried
    )
    offset = jnp.einsum("...jd,...jv->...dv", weighted, writes, precision=HIGHEST)
    return (local_out, query_eff, transition, offset)


def apply_map(transition, offset, state_in):
    return jnp.einsum("hij,hjv->hiv", transition, state_in, precision=HIGHEST) + offset


def local(
    queries,
    keys,
    values,
    out_gate,
    write_rate,
    decay,
    head_gain,
    residual,
    out_proj,
    ffn_gain,
    expert_ids,
    route_weight,
    w_gate,
    w_up,
    w_down,
    ablate_mask,
    direction,
):
    tokens_here = queries.shape[1]
    group_size = CONTENT_MIXERS // KH
    query_raw = jnp.repeat(
        queries[0].astype(jnp.float32).reshape(tokens_here, KH, DK), group_size, axis=1
    ).transpose(1, 0, 2)
    query_f = (
        query_raw
        / jnp.sqrt(jnp.sum(query_raw * query_raw, -1, keepdims=True) + 1e-06)
        * DK ** (-0.5)
    )
    key_f = jnp.repeat(
        keys[0].astype(jnp.float32).reshape(tokens_here, KH, DK), group_size, axis=1
    ).transpose(1, 0, 2)
    key_unit = key_f / jnp.sqrt(jnp.sum(key_f * key_f, -1, keepdims=True) + 1e-06)
    value_f = (
        values[0].astype(jnp.float32).reshape(tokens_here, CONTENT_MIXERS, DV).transpose(1, 0, 2)
    )
    write_f = write_rate[0].T
    decay_f = decay[0].T
    local_out, query_eff, transition, offset = block_maps(
        query_f, key_unit, value_f, write_f, decay_f
    )
    zero_state = jnp.zeros((CONTENT_MIXERS, DK, DV), jnp.float32)

    def relay_turn(turn_index, incoming):
        outgoing = apply_map(transition, offset, incoming)
        return passed_along(outgoing, "ctx", 1)

    state_in = lax.fori_loop(0, lax.axis_size("ctx") - 1, relay_turn, zero_state)
    head_out = local_out + jnp.einsum("hid,hdv->hiv", query_eff, state_in, precision=HIGHEST)
    mean_square = jnp.mean(head_out * head_out, -1, keepdims=True)
    gate_f = (
        out_gate[0].astype(jnp.float32).reshape(tokens_here, CONTENT_MIXERS, DV).transpose(1, 0, 2)
    )
    normed = head_out / jnp.sqrt(mean_square + 1e-06) * head_gain * jax.nn.silu(gate_f)
    mixed = normed.transpose(1, 0, 2).reshape(tokens_here, CONTENT_MIXERS * DV).astype(jnp.bfloat16)
    projected = jnp.dot(
        mixed,
        lax.all_gather(out_proj, "ctx", axis=0, tiled=True),
        preferred_element_type=jnp.float32,
    )
    hidden_sum = residual[0].astype(jnp.float32) + projected
    ffn_in = (
        hidden_sum
        / jnp.sqrt(jnp.mean(hidden_sum * hidden_sum, -1, keepdims=True) + 1e-06)
        * ffn_gain
    ).astype(jnp.bfloat16)
    chain_devices = lax.axis_size("ctx")
    owner_devices = lax.axis_size("exp")
    window_experts = chain_devices * owner_devices
    flat_ids = expert_ids[0].reshape(-1)
    expert_range = jnp.arange(window_experts, dtype=jnp.int32)
    one_hot = (flat_ids[:, None] == expert_range[None, :]).astype(jnp.int32)
    slot_index = jnp.sum(jnp.cumsum(one_hot, axis=0) * one_hot, axis=1) - 1
    in_window = flat_ids < window_experts
    dropped = window_experts * CAP
    destination = jnp.where(in_window, flat_ids * CAP + slot_index, dropped)
    token_of = jnp.arange(flat_ids.shape[0], dtype=jnp.int32) // TOP
    outgoing_rows = (
        jnp.zeros((dropped, D), jnp.bfloat16).at[destination].set(ffn_in[token_of], mode="drop")
    )
    outgoing_rows = outgoing_rows.reshape(chain_devices, owner_devices, CAP, D)
    arrived = lax.all_to_all(
        lax.all_to_all(outgoing_rows, "exp", split_axis=1, concat_axis=1, tiled=True),
        "ctx",
        split_axis=0,
        concat_axis=0,
        tiled=True,
    )
    expert_rows = arrived.reshape(-1, D)
    gate_part = jnp.dot(expert_rows, w_gate[0], preferred_element_type=jnp.float32)
    up_part = jnp.dot(expert_rows, w_up[0], preferred_element_type=jnp.float32)
    activated = (jax.nn.silu(gate_part) * up_part).astype(jnp.bfloat16)
    expert_out = jnp.dot(activated, w_down[0], preferred_element_type=jnp.float32).astype(
        jnp.bfloat16
    )
    expert_out = expert_out.reshape(chain_devices, owner_devices, CAP, D)
    returned = lax.all_to_all(
        lax.all_to_all(expert_out, "exp", split_axis=1, concat_axis=1, tiled=True),
        "ctx",
        split_axis=0,
        concat_axis=0,
        tiled=True,
    )
    returned_rows = returned.reshape(-1, D)
    picked = returned_rows[jnp.minimum(destination, dropped - 1)]
    pair_weight = jnp.where(in_window, route_weight[0].reshape(-1), 0.0)
    moe_sum = jnp.sum(
        (pair_weight[:, None] * picked.astype(jnp.float32)).reshape(tokens_here, TOP, D), axis=1
    )
    combined = hidden_sum + moe_sum
    unit_dir = direction / jnp.sqrt(jnp.sum(direction * direction) + 1e-06)
    along = jnp.dot(combined, unit_dir, precision=HIGHEST)
    mask_f = ablate_mask[0].astype(jnp.float32)
    layer_out = combined - (mask_f * along)[:, None] * unit_dir[None, :]
    return layer_out.astype(jnp.bfloat16)[None]


def solution(mesh):
    placed = (
        P("exp", "ctx", None),
        P("exp", "ctx", None),
        P("exp", "ctx", None),
        P("exp", "ctx", None),
        P("exp", "ctx", None),
        P("exp", "ctx", None),
        P(),
        P("exp", "ctx", None),
        P("ctx", None),
        P(),
        P("exp", "ctx", None),
        P("exp", "ctx", None),
        P(("ctx", "exp"), None, None),
        P(("ctx", "exp"), None, None),
        P(("ctx", "exp"), None, None),
        P("exp", "ctx"),
        P(),
    )
    return jax.shard_map(
        local, mesh=mesh, in_specs=placed, out_specs=P("exp", "ctx", None), check_vma=False
    )
```

profile of v0, /device:TPU:5, one launch (start us, length us, event | category | flops | bytes accessed | tf_op | source)
XLA Modules:
  0.0 813.5 jit_solution(2493957062521577423)
XLA Ops:
  17.0 158.6 %custom-call.4 = f32[16,1,128,128]{2,3,1,0:T(8,128)} custom-call(f32[16,1,128,128]{3,2,1,0:T(8,128)} %fusion.15), custom_call_target="InvertDiagBlocksLowerTriangular" | custom-call | tf_op jit(solution)/shard_map/jit(_solve_triangular)/vmap()/triangular_solve | solution.py:38
  209.7 139.4 %while.10 = (s32[]{:T(128)}, f32[16,128,128]{2,1,0:T(8,128)S(1)}, f32[16,128,128]{2,1,0:T(8,128)}, f32[16,128,128]{2,1,0:T(8,128)}, s32[]{:T(128)}) while((s32[]{:T(128)}, f32[16,128,128]{2,1,0:T(8,128)S(1)}, f32[16,128,128]{2,1,0:T(8,128)}, f32[16,128,128]{2,1,0:T(8,128)}, s32[]{:T(128)}) %tuple.27), condition=%wide.region_4.6_spmd, body=%wide.region_3.5_spmd.sunk | while | flops 402915328 | bytes 8388709 | solution.py:110
  217.2 12.0 %collective-permute-done = f32[16,128,128]{2,1,0:T(8,128)S(1)} collective-permute-done((f32[16,128,128]{2,1,0:T(8,128)}, f32[16,128,128]{2,1,0:T(8,128)S(1)}, u32[]{:S(2)}, u32[]{:S(2)}) %collective-permute-start) | collective-permute-done | bytes 1048608 | tf_op jit(solution)/shard_map/while/body/eval_jaxpr/ppermute | solution.py:21
  237.2 12.0 %collective-permute-done = f32[16,128,128]{2,1,0:T(8,128)S(1)} collective-permute-done((f32[16,128,128]{2,1,0:T(8,128)}, f32[16,128,128]{2,1,0:T(8,128)S(1)}, u32[]{:S(2)}, u32[]{:S(2)}) %collective-permute-start) | collective-permute-done | bytes 1048608 | tf_op jit(solution)/shard_map/while/body/eval_jaxpr/ppermute | solution.py:21
  257.1 12.0 %collective-permute-done = f32[16,128,128]{2,1,0:T(8,128)S(1)} collective-permute-done((f32[16,128,128]{2,1,0:T(8,128)}, f32[16,128,128]{2,1,0:T(8,128)S(1)}, u32[]{:S(2)}, u32[]{:S(2)}) %collective-permute-start) | collective-permute-done | bytes 1048608 | tf_op jit(solution)/shard_map/while/body/eval_jaxpr/ppermute | solution.py:21
  277.1 12.0 %collective-permute-done = f32[16,128,128]{2,1,0:T(8,128)S(1)} collective-permute-done((f32[16,128,128]{2,1,0:T(8,128)}, f32[16,128,128]{2,1,0:T(8,128)S(1)}, u32[]{:S(2)}, u32[]{:S(2)}) %collective-permute-start) | collective-permute-done | bytes 1048608 | tf_op jit(solution)/shard_map/while/body/eval_jaxpr/ppermute | solution.py:21
  297.1 12.0 %collective-permute-done = f32[16,128,128]{2,1,0:T(8,128)S(1)} collective-permute-done((f32[16,128,128]{2,1,0:T(8,128)}, f32[16,128,128]{2,1,0:T(8,128)S(1)}, u32[]{:S(2)}, u32[]{:S(2)}) %collective-permute-start) | collective-permute-done | bytes 1048608 | tf_op jit(solution)/shard_map/while/body/eval_jaxpr/ppermute | solution.py:21
  317.1 12.0 %collective-permute-done = f32[16,128,128]{2,1,0:T(8,128)S(1)} collective-permute-done((f32[16,128,128]{2,1,0:T(8,128)}, f32[16,128,128]{2,1,0:T(8,128)S(1)}, u32[]{:S(2)}, u32[]{:S(2)}) %collective-permute-start) | collective-permute-done | bytes 1048608 | tf_op jit(solution)/shard_map/while/body/eval_jaxpr/ppermute | solution.py:21
  337.1 12.0 %collective-permute-done = f32[16,128,128]{2,1,0:T(8,128)S(1)} collective-permute-done((f32[16,128,128]{2,1,0:T(8,128)}, f32[16,128,128]{2,1,0:T(8,128)S(1)}, u32[]{:S(2)}, u32[]{:S(2)}) %collective-permute-start) | collective-permute-done | bytes 1048608 | tf_op jit(solution)/shard_map/while/body/eval_jaxpr/ppermute | solution.py:21
  359.8 34.5 %scatter_custom_fusion = bf16[1024,2048]{1,0:T(8,128)(2,1)} fusion(s32[1280]{0:T(1024)S(1)} %get-tuple-element.30, bf16[128,2048]{1,0:T(8,128)(2,1)} %multiply_convert_fusion.1, s32[2048]{0:T(1024)S(1)} %pad_clamp_fusion.1, bf16[]{:T(256)} %constant.56.clone.1), kind=kCustom, calls=%fused_computation.5 | custom fusion | bytes 4194816 | tf_op jit(solution)/shard_map/scatter | solution.py:141
  394.3 7.3 reshape.283
  405.9 103.5 %all_to_all.20 = bf16[8,32,4,2048]{3,2,0,1:T(4,128)(2,1)S(1)} all-to-all(bf16[8,32,4,2048]{3,2,0,1:T(4,128)(2,1)S(1)} %copy.113), channel_id=1, replica_groups=mesh['ctx'=8,'exp'=32] {'exp'}, dimensions={1} | all-to-all | bytes 8388608 | tf_op jit(solution)/shard_map/all_to_all | solution.py:145
  512.3 56.0 %all_to_all.21 = bf16[8,32,4,2048]{3,2,1,0:T(4,128)(2,1)} all-to-all(bf16[8,32,4,2048]{3,2,1,0:T(4,128)(2,1)S(1)} %copy.114), channel_id=1, replica_groups=mesh['ctx'=8,'exp'=32] {'ctx'}, dimensions={0} | all-to-all | bytes 8388608 | tf_op jit(solution)/shard_map/all_to_all | solution.py:144
  568.3 6.9 reshape.284
  575.2 6.6 fusion.3
  581.8 10.1 %convolution_convert_fusion = bf16[1024,2048]{1,0:T(8,128)(2,1)} fusion(bf16[1,512,2048]{2,1,0:T(8,128)(2,1)S(1)} %copy-done, f32[1024,512]{1,0:T(8,128)} %fusion.3, bf16[1024,2048]{1,0:T(8,128)(2,1)} %reshape.284, bf16[1,2048,512]{2,1,0:T(8,128)(2,1)} %param.33), kind=kOutput, calls=%fused_computation.7 | convolution fusion | flops 4300210176 | bytes 14680064 | tf_op jit(solution)/shard_map/dot_general | solution.py:155
  591.9 7.2 reshape.285
  603.3 97.0 %all_to_all.22 = bf16[8,32,4,2048]{3,2,0,1:T(4,128)(2,1)S(1)} all-to-all(bf16[8,32,4,2048]{3,2,0,1:T(4,128)(2,1)S(1)} %copy.115), channel_id=1, replica_groups=mesh['ctx'=8,'exp'=32] {'exp'}, dimensions={1} | all-to-all | bytes 8388608 | tf_op jit(solution)/shard_map/all_to_all | solution.py:160
  704.4 11.0 %all-to-all-start.3 = ((bf16[8,32,4,2048]{3,2,1,0:T(4,128)(2,1)}), bf16[8,32,4,2048]{3,2,1,0:T(4,128)(2,1)}, u32[]{:S(2)}, u32[]{:S(2)}) async-start(bf16[8,32,4,2048]{3,2,1,0:T(4,128)(2,1)} %copy.116), calls=%async_computation.3 | async-start | bytes 8388608 | tf_op jit(solution)/shard_map/all_to_all | solution.py:159
  716.9 44.8 %all-to-all-done.3 = bf16[8,32,4,2048]{3,2,1,0:T(4,128)(2,1)} async-done(((bf16[8,32,4,2048]{3,2,1,0:T(4,128)(2,1)}), bf16[8,32,4,2048]{3,2,1,0:T(4,128)(2,1)}, u32[]{:S(2)}, u32[]{:S(2)}) %all-to-all-start.3) | async-done | bytes 4194336 | tf_op jit(solution)/shard_map/all_to_all | solution.py:159
  761.7 6.9 reshape.286
  768.6 13.6 %gather_fusion = bf16[1280,2048]{1,0:T(8,128)(2,1)} fusion(bf16[1024,2048]{1,0:T(8,128)(2,1)} %reshape.286, s32[2048]{0:T(1024)S(1)} %pad_clamp_fusion), kind=kCustom, calls=%fused_computation.1 | custom fusion | bytes 10490880 | tf_op jit(solution)/shard_map/gather | solution.py:167
  782.2 10.4 %reshape.291 = f32[128,10,2048]{2,1,0:T(8,128)} reshape(bf16[1280,2048]{1,0:T(8,128)(2,1)} %gather_fusion) | data formatting | bytes 15728640 | tf_op jit(solution)/shard_map/convert_element_type | solution.py:170
  792.6 10.7 %multiply_reduce_fusion = f32[128,2048]{1,0:T(8,128)} fusion(f32[128,10,2048]{2,1,0:T(8,128)} %reshape.291, f32[128,10]{1,0:T(8,128)S(1)} %bitcast.119), kind=kLoop, calls=%fused_computation.4 | loop fusion | flops 4980736 | bytes 11539456 | tf_op jit(solution)/shard_map/reduce_sum | solution.py:169
  (120 shorter events, 129.0 us)
Async XLA Ops:
  6.5 575.2 %copy-start = (bf16[1,512,2048]{2,1,0:T(8,128)(2,1)S(1)}, bf16[1,512,2048]{2,1,0:T(8,128)(2,1)}, u32[]{:S(2)}) copy-start(bf16[1,512,2048]{2,1,0:T(8,128)(2,1)} %param.35) | copy-start | bytes 6291460
  6.5 7.1 copy-start.9
  6.5 347.3 %all-gather.2.cloned.1.call-start = ((), (), s32[]{:S(2)}) async-start(), calls=%async_computation.4 | async-start | bytes 9437184 | tf_op jit(solution)/shard_map/all_gather | solution.py:120
  10.6 169.3 %copy-start.7 = (bf16[1,128,1024]{2,1,0:T(8,128)(2,1)S(1)}, bf16[1,128,1024]{2,1,0:T(8,128)(2,1)}, u32[]{:S(2)}) copy-start(bf16[1,128,1024]{2,1,0:T(8,128)(2,1)} %param.21) | copy-start | bytes 786436
  179.9 4.2 copy-start.10
  186.0 3.8 copy-start.8
  186.0 5.1 copy-start.12
  190.4 6.3 copy-start.2
  192.9 8.1 copy-start.5
  213.8 15.4 %collective-permute-start = (f32[16,128,128]{2,1,0:T(8,128)}, f32[16,128,128]{2,1,0:T(8,128)S(1)}, u32[]{:S(2)}, u32[]{:S(2)}) collective-permute-start(f32[16,128,128]{2,1,0:T(8,128)} %convolution_add_fusion.4), channel_id=1, source_target_pairs={{0,32},{32,64},{64,96},{96,128},{128,160},{160,192},{192,224},{1,3... | collective-permute-start | bytes 3145736 | tf_op jit(solution)/shard_map/while/body/eval_jaxpr/ppermute | solution.py:21
  232.9 16.3 %collective-permute-start = (f32[16,128,128]{2,1,0:T(8,128)}, f32[16,128,128]{2,1,0:T(8,128)S(1)}, u32[]{:S(2)}, u32[]{:S(2)}) collective-permute-start(f32[16,128,128]{2,1,0:T(8,128)} %convolution_add_fusion.4), channel_id=1, source_target_pairs={{0,32},{32,64},{64,96},{96,128},{128,160},{160,192},{192,224},{1,3... | collective-permute-start | bytes 3145736 | tf_op jit(solution)/shard_map/while/body/eval_jaxpr/ppermute | solution.py:21
  252.9 16.3 %collective-permute-start = (f32[16,128,128]{2,1,0:T(8,128)}, f32[16,128,128]{2,1,0:T(8,128)S(1)}, u32[]{:S(2)}, u32[]{:S(2)}) collective-permute-start(f32[16,128,128]{2,1,0:T(8,128)} %convolution_add_fusion.4), channel_id=1, source_target_pairs={{0,32},{32,64},{64,96},{96,128},{128,160},{160,192},{192,224},{1,3... | collective-permute-start | bytes 3145736 | tf_op jit(solution)/shard_map/while/body/eval_jaxpr/ppermute | solution.py:21
  272.8 16.3 %collective-permute-start = (f32[16,128,128]{2,1,0:T(8,128)}, f32[16,128,128]{2,1,0:T(8,128)S(1)}, u32[]{:S(2)}, u32[]{:S(2)}) collective-permute-start(f32[16,128,128]{2,1,0:T(8,128)} %convolution_add_fusion.4), channel_id=1, source_target_pairs={{0,32},{32,64},{64,96},{96,128},{128,160},{160,192},{192,224},{1,3... | collective-permute-start | bytes 3145736 | tf_op jit(solution)/shard_map/while/body/eval_jaxpr/ppermute | solution.py:21
  292.8 16.3 %collective-permute-start = (f32[16,128,128]{2,1,0:T(8,128)}, f32[16,128,128]{2,1,0:T(8,128)S(1)}, u32[]{:S(2)}, u32[]{:S(2)}) collective-permute-start(f32[16,128,128]{2,1,0:T(8,128)} %convolution_add_fusion.4), channel_id=1, source_target_pairs={{0,32},{32,64},{64,96},{96,128},{128,160},{160,192},{192,224},{1,3... | collective-permute-start | bytes 3145736 | tf_op jit(solution)/shard_map/while/body/eval_jaxpr/ppermute | solution.py:21
  312.8 16.3 %collective-permute-start = (f32[16,128,128]{2,1,0:T(8,128)}, f32[16,128,128]{2,1,0:T(8,128)S(1)}, u32[]{:S(2)}, u32[]{:S(2)}) collective-permute-start(f32[16,128,128]{2,1,0:T(8,128)} %convolution_add_fusion.4), channel_id=1, source_target_pairs={{0,32},{32,64},{64,96},{96,128},{128,160},{160,192},{192,224},{1,3... | collective-permute-start | bytes 3145736 | tf_op jit(solution)/shard_map/while/body/eval_jaxpr/ppermute | solution.py:21
  332.8 16.3 %collective-permute-start = (f32[16,128,128]{2,1,0:T(8,128)}, f32[16,128,128]{2,1,0:T(8,128)S(1)}, u32[]{:S(2)}, u32[]{:S(2)}) collective-permute-start(f32[16,128,128]{2,1,0:T(8,128)} %convolution_add_fusion.4), channel_id=1, source_target_pairs={{0,32},{32,64},{64,96},{96,128},{128,160},{160,192},{192,224},{1,3... | collective-permute-start | bytes 3145736 | tf_op jit(solution)/shard_map/while/body/eval_jaxpr/ppermute | solution.py:21
  349.1 3.5 copy-start.6
  349.1 3.5 copy-start.16
  353.8 5.0 copy-start.13
  704.4 11.1 %copy-start.14 = (f32[1,128,10]{1,0,2:T(1,128)S(1)}, f32[1,128,10]{1,0,2:T(1,128)}, u32[]{:S(2)}) copy-start(f32[1,128,10]{1,0,2:T(1,128)} %param.32) | copy-start | bytes 15364
  704.4 11.2 %copy-start.11 = (f32[2048]{0:T(1024)S(1)}, f32[2048]{0:T(1024)}, u32[]{:S(2)}) copy-start(f32[2048]{0:T(1024)} %param.37) | copy-start | bytes 24580
  704.4 57.3 %all-to-all-start.3 = ((bf16[8,32,4,2048]{3,2,1,0:T(4,128)(2,1)}), bf16[8,32,4,2048]{3,2,1,0:T(4,128)(2,1)}, u32[]{:S(2)}, u32[]{:S(2)}) async-start(bf16[8,32,4,2048]{3,2,1,0:T(4,128)(2,1)} %copy.116), calls=%async_computation.3 | async-start | bytes 8388608 | tf_op jit(solution)/shard_map/all_to_all | solution.py:159
  792.6 12.0 %copy-start.15 = (s32[1,128]{1,0:T(1,128)S(1)}, s32[1,128]{1,0:T(1,128)}, u32[]{:S(2)}) copy-start(s32[1,128]{1,0:T(1,128)} %param.36) | copy-start | bytes 1540
  792.6 13.9 %copy-start.1 = (bf16[1,512,2048]{2,1,0:T(8,128)(2,1)S(1)}, bf16[1,512,2048]{2,1,0:T(8,128)(2,1)}, u32[]{:S(2)}) copy-start(bf16[1,512,2048]{2,1,0:T(8,128)(2,1)} %param.35) | copy-start | bytes 6291460
  (2 other events, 2.2 us)
Sparse Core Ops, SparseCore 0:
  9.2 54.7 all-gather.1
where the time goes:
time: 825 us; the launch traced here: 814 us
  blocking collectives  257 us (31%)
  other arithmetic  182 us (22%)
  waiting for transfers between devices  130 us (16%)
  local copies, waits for them, and re-layouts  118 us (14%)
  matrix products  71.7 us (9%)
  starting transfers between devices  40 us (5%)
  between operations  14.7 us (2%)
    another operation x4, other arithmetic, block_maps(): jax.scipy.linalg.solve_triangular(system, write_f[..., None] * value_f, l...  159 us
    all_to_all x1, blocking collectives, local(): lax.all_to_all(outgoing_rows, 'exp', split_axis=1, concat_axis=1, tiled=T...  103 us
    all_to_all x1, blocking collectives, local(): lax.all_to_all(expert_out, 'exp', split_axis=1, concat_axis=1, tiled=True)  97 us
    ppermute x7, waiting for transfers between devices, passed_along(): return lax.ppermute(block, axis, route)  84.2 us
    all_to_all x1, blocking collectives, local(): lax.all_to_all(lax.all_to_all(outgoing_rows, 'exp', split_axis=1, concat_...  56 us
    all_to_all x1, waiting for transfers between devices, local(): lax.all_to_all(lax.all_to_all(expert_out, 'exp', split_axis=1, concat_axi...  44.8 us
    scatter x1, local copies, waits for them, and re-layouts, local(): jnp.zeros((dropped, D), jnp.bfloat16).at[destination]  34.5 us
    ppermute x7, starting transfers between devices, passed_along(): return lax.ppermute(block, axis, route)  29 us
  transfers between devices with their start and end apart: 9, of which 8 were waited for; matrix products, arithmetic and copies ran while one was open for 28% of the time, Pallas kernels for 0%

commit v1 on v0

v1 whole, which is shorter than its diff:
```python
import jax
import jax.numpy as jnp
from jax import lax
from jax.experimental import pallas as pl
from jax.experimental.pallas import tpu as pltpu
from jax.sharding import PartitionSpec as P

D = 2048
HEADS = 16
KH = 8
DK = 128
DV = 128
T = 128
TOP = 10
CAP = 4
N_CTX = 8
STATE = jnp.float32
F32 = jnp.float32
BF16 = jnp.bfloat16
HIGHEST = lax.Precision.HIGHEST
MESH = pl.DeviceIdType.MESH


def split(a, parts):
    if a.dtype == BF16:
        return [a]
    pieces = []
    for _ in range(parts):
        piece = a.astype(BF16)
        pieces.append(piece)
        a = a - piece.astype(F32)
    return pieces


def mm(a, b, na=1, nb=1):
    total = None
    for i, x in enumerate(split(a, na)):
        for j, y in enumerate(split(b, nb)):
            if i + j < max(na, nb):
                term = jnp.dot(x, y, preferred_element_type=F32)
                total = term if total is None else total + term
    return total


def mm_t(a, b):
    return lax.dot_general(a, b, (((1,), (1,)), ((), ())), preferred_element_type=F32)


def mixer_kernel(
    q_ref, k_ref, v_ref, gate_ref, w_ref, wt_ref, d_ref, dt_ref, gain_ref, out_ref,
    lc_ref, lr_ref, loc_ref, qeff_ref, car_ref, off_ref, got_ref, sent_ref, send_sem, recv_sem,
):
    me = lax.axis_index("ctx")
    last = N_CTX - 1
    barrier = pltpu.get_barrier_semaphore()

    @pl.when(me > 0)
    def _():
        pl.semaphore_signal(barrier, inc=1, device_id={"ctx": me - 1}, device_id_type=MESH)

    @pl.when(me < last)
    def _():
        pl.semaphore_signal(barrier, inc=1, device_id={"ctx": me + 1}, device_id_type=MESH)

    rows = lax.broadcasted_iota(jnp.int32, (T, T), 0)
    cols = lax.broadcasted_iota(jnp.int32, (T, T), 1)
    lower = (rows >= cols).astype(F32)
    upper = (rows <= cols).astype(F32)
    eye = (rows == cols).astype(F32)
    lc_ref[...] = jnp.dot(lower, jnp.log(d_ref[...]), precision=HIGHEST, preferred_element_type=F32)
    lr_ref[...] = jnp.dot(jnp.log(dt_ref[...]), upper, precision=HIGHEST, preferred_element_type=F32)
    ones = jnp.ones((8, DK), F32)
    head_lane = lax.broadcasted_iota(jnp.int32, (T, HEADS), 1)
    in_16 = (rows // 16 == cols // 16) & (rows > cols)

    def column(array, h):
        return jnp.sum(jnp.where(head_lane == h, array, 0.0), axis=1, keepdims=True)

    def maps(step, carry):
        groups = [step * 2, step * 2 + 1]
        per_group = []
        for g in groups:
            at = pl.ds(pl.multiple_of(g * DK, DK), DK)
            kraw, qraw = k_ref[:, at], q_ref[:, at]
            kf, qf = kraw.astype(F32), qraw.astype(F32)
            ksq = kf * kf
            rk = lax.rsqrt(jnp.sum(ksq, axis=1, keepdims=True) + 1e-06)
            rk_row = lax.rsqrt(
                lax.dot_general(
                    ones, ksq, (((1,), (1,)), ((), ())), precision=HIGHEST, preferred_element_type=F32
                )[0:1] + 1e-06
            )
            rq = lax.rsqrt(jnp.sum(qf * qf, axis=1, keepdims=True) + 1e-06) * DK ** (-0.5)
            kk = mm_t(kraw, kraw) * rk * rk_row
            qk = mm_t(qraw, kraw) * rq * rk_row
            kt = kf.T * rk_row
            per_group.append((kraw, qf * rq, rk_row, kk, qk, kt))
        heads = []
        for i, g in enumerate(groups):
            for j in range(2):
                heads.append((per_group[i], g * 2 + j))
        state = []
        for (kraw, qu, rk_row, kk, qk, kt), h in heads:
            lcol = column(lc_ref[...], h)
            wcol = column(w_ref[...], h)
            lrow = lr_ref[pl.ds(h, 1), :]
            wrow = wt_ref[pl.ds(h, 1), :]
            ratio = jnp.exp(jnp.minimum(lcol - lrow, 0.0)) * lower
            a = jnp.where(rows > cols, ratio * kk, 0.0) * wcol
            remain = jnp.exp(lrow[:, T - 1 : T] - lrow)
            g2 = jnp.concatenate([qk * ratio, kt * remain], axis=0)
            state.append((a, g2, wrow, wrow * jnp.exp(lrow) * rk_row, jnp.exp(lcol)))
        n = range(len(heads))
        a = [s[0] for s in state]
        dg = [jnp.where(in_16, x, 0.0) for x in a]
        d2 = [mm(x, x) for x in dg]
        d3 = [mm(dg[i], d2[i]) for i in n]
        d4 = [mm(x, x) for x in d2]
        m1 = [eye - dg[i] + d2[i] - d3[i] for i in n]
        d8 = [mm(x, x) for x in d4]
        m2 = [m1[i] + mm(m1[i], d4[i]) for i in n]
        inv = [m2[i] + mm(m2[i], d8[i]) for i in n]
        for size in (16, 32, 64):
            band = (rows // (2 * size) == cols // (2 * size)) & (rows // size > cols // size)
            part = [jnp.where(band, x, 0.0) for x in a]
            half = [mm(part[i], inv[i]) for i in n]
            inv = [inv[i] - mm(inv[i], half[i]) for i in n]
        y = [mm(state[i][1], inv[i], 2, 2) for i in n]
        for i in n:
            (kraw, qu, rk_row, kk, qk, kt), h = heads[i]
            _, _, w1, w2, cum = state[i]
            vraw = v_ref[:, pl.ds(pl.multiple_of(h * DV, DV), DV)]
            z1 = mm(y[i] * w1, vraw, 2)
            z2 = mm(y[i] * w2, kraw, 2)
            loc_ref[h] = z1[:T]
            off_ref[h] = z1[T:]
            qeff_ref[h] = cum * qu - z2[:T]
            car_ref[h] = z2[T:]
        return carry

    lax.fori_loop(0, KH // 2, maps, 0)

    @pl.when((me > 0) & (me < last))
    def _():
        pl.semaphore_wait(barrier, 2)

    @pl.when((me == 0) | (me == last))
    def _():
        pl.semaphore_wait(barrier, 1)

    def hop(h):
        return pltpu.make_async_remote_copy(
            src_ref=sent_ref.at[h],
            dst_ref=got_ref.at[h],
            send_sem=send_sem.at[h],
            recv_sem=recv_sem.at[h],
            device_id={"ctx": jnp.minimum(me + 1, last)},
            device_id_type=MESH,
        )

    def fraction(h):
        return jnp.exp(lr_ref[pl.ds(h, 1), T - 1 : T])

    @pl.when(me == 0)
    def _():
        def start(h, carry):
            got_ref[h] = jnp.zeros((DK, DV), STATE)
            sent_ref[h] = off_ref[h].astype(STATE)
            hop(h).start()
            return carry

        lax.fori_loop(0, HEADS, start, 0)

    @pl.when((me > 0) & (me < last))
    def _():
        def relay(h, carry):
            hop(h).wait_recv()
            s = got_ref[h].astype(F32)
            sent_ref[h] = (fraction(h) * s + off_ref[h] - mm(car_ref[h], s, 2, 2)).astype(STATE)
            hop(h).start()
            return carry

        lax.fori_loop(0, HEADS, relay, 0)

    gain = gain_ref[...]

    def finish(h, carry):
        @pl.when(me == last)
        def _():
            hop(h).wait_recv()

        o = loc_ref[h] + mm(qeff_ref[h], got_ref[h].astype(F32), 2, 2)
        at = pl.ds(pl.multiple_of(h * DV, DV), DV)
        gate = gate_ref[:, at].astype(F32)
        scale = lax.rsqrt(jnp.mean(o * o, axis=1, keepdims=True) + 1e-06)
        out_ref[:, at] = (o * scale * gain * (gate / (1.0 + jnp.exp(-gate)))).astype(BF16)
        return carry

    lax.fori_loop(0, HEADS, finish, 0)

    @pl.when(me < last)
    def _():
        def drain(h, carry):
            hop(h).wait_send()
            return carry

        lax.fori_loop(0, HEADS, drain, 0)


def mixer(queries, keys, values, out_gate, write_rate, decay, head_gain):
    square = pltpu.VMEM((HEADS, DK, DV), F32)
    return pl.pallas_call(
        mixer_kernel,
        out_shape=jax.ShapeDtypeStruct((T, HEADS * DV), BF16),
        in_specs=[pl.BlockSpec(memory_space=pltpu.VMEM)] * 9,
        out_specs=pl.BlockSpec(memory_space=pltpu.VMEM),
        scratch_shapes=[
            pltpu.VMEM((T, HEADS), F32),
            pltpu.VMEM((HEADS, T), F32),
            square, square, square, square,
            pltpu.VMEM((HEADS, DK, DV), STATE),
            pltpu.VMEM((HEADS, DK, DV), STATE),
            pltpu.SemaphoreType.DMA((HEADS,)),
            pltpu.SemaphoreType.DMA((HEADS,)),
        ],
        compiler_params=pltpu.CompilerParams(
            collective_id=0, has_side_effects=True, vmem_limit_bytes=40 * 2**20
        ),
        cost_estimate=pl.CostEstimate(flops=20 * 10**9, bytes_accessed=2 * 10**6, transcendentals=0),
        name="mixer",
    )(queries, keys, values, out_gate, write_rate, write_rate.T, decay, decay.T, head_gain[None, :])


def local(
    queries, keys, values, out_gate, write_rate, decay, head_gain, residual, out_proj, ffn_gain,
    expert_ids, route_weight, w_gate, w_up, w_down, ablate_mask, direction,
):
    mixed = mixer(queries[0], keys[0], values[0], out_gate[0], write_rate[0], decay[0], head_gain)
    projected = jnp.dot(
        mixed, lax.all_gather(out_proj, "ctx", axis=0, tiled=True), preferred_element_type=F32
    )
    hidden_sum = residual[0].astype(F32) + projected
    ffn_in = (
        hidden_sum / jnp.sqrt(jnp.mean(hidden_sum * hidden_sum, -1, keepdims=True) + 1e-06) * ffn_gain
    ).astype(BF16)
    n_ctx, n_exp = lax.axis_size("ctx"), lax.axis_size("exp")
    window = n_ctx * n_exp
    ids = expert_ids[0]
    named = ids[:, :, None] == jnp.arange(window, dtype=jnp.int32)[None, None, :]
    member = jnp.sum(named.astype(F32), axis=1)
    weight = jnp.sum(jnp.where(named, route_weight[0][:, :, None], 0.0), axis=1)
    earlier = jnp.tril(jnp.ones((T, T), F32), -1)
    slot = jnp.dot(earlier, member, preferred_element_type=F32)
    slots = jnp.arange(CAP, dtype=F32)
    taken = (slot[:, :, None] == slots) & (member[:, :, None] > 0)
    pick = taken.astype(BF16).reshape(T, window * CAP)
    weights = jnp.where(taken, weight[:, :, None], 0.0).reshape(T, window * CAP)
    outgoing = jnp.dot(pick.T, ffn_in, preferred_element_type=F32).astype(BF16)
    outgoing = outgoing.reshape(n_ctx, n_exp, CAP, D)

    def exchange(rows):
        rows = lax.all_to_all(rows, "exp", split_axis=1, concat_axis=1, tiled=True)
        return lax.all_to_all(rows, "ctx", split_axis=0, concat_axis=0, tiled=True)

    rows = exchange(outgoing).reshape(-1, D)
    gate_part = jnp.dot(rows, w_gate[0], preferred_element_type=F32)
    up_part = jnp.dot(rows, w_up[0], preferred_element_type=F32)
    act = (jax.nn.silu(gate_part) * up_part).astype(BF16)
    expert_out = jnp.dot(act, w_down[0], preferred_element_type=F32).astype(BF16)
    returned = exchange(expert_out.reshape(n_ctx, n_exp, CAP, D)).reshape(-1, D)
    high = weights.astype(BF16)
    rest = (weights - high.astype(F32)).astype(BF16)
    moe_sum = jnp.dot(high, returned, preferred_element_type=F32) + jnp.dot(
        rest, returned, preferred_element_type=F32
    )
    combined = hidden_sum + moe_sum
    unit_dir = direction / jnp.sqrt(jnp.sum(direction * direction) + 1e-06)
    along = jnp.sum(combined * unit_dir[None, :], axis=1)
    mask_f = ablate_mask[0].astype(F32)
    layer_out = combined - (mask_f * along)[:, None] * unit_dir[None, :]
    return layer_out.astype(BF16)[None]


def solution(mesh):
    tokens = P("exp", "ctx", None)
    experts = P(("ctx", "exp"), None, None)
    placed = (
        tokens, tokens, tokens, tokens, tokens, tokens, P(), tokens, P("ctx", None), P(),
        tokens, tokens, experts, experts, experts, P("exp", "ctx"), P(),
    )
    return jax.shard_map(local, mesh=mesh, in_specs=placed, out_specs=tokens, check_vma=False)
```

time: 825 us -> 476 us (0.58)
  other arithmetic: 182 us -> 3.22 us
  waiting for transfers between devices: 130 us -> 44.9 us
  local copies, waits for them, and re-layouts: 118 us -> 54.7 us
  Pallas kernels: 0 us -> 60.2 us
  matrix products: 71.7 us -> 28.9 us
  starting transfers between devices: 40 us -> 10.8 us
    another operation x8 -> x0, other arithmetic: 161 us -> none  [the longest x4 159 us: block_maps(): jax.scipy.linalg.solve_triangular(system, write_f[..., None] * value_f, l...]
    ppermute x7 -> x0, waiting for transfers between devices: 84.2 us -> none  [passed_along(): return lax.ppermute(block, axis, route)]
    pallas_call x0 -> x1, Pallas kernels: none -> 60.2 us  [mixer(): pl.pallas_call(mixer_kernel, out_shape=jax.ShapeDtypeStruct((T, HEADS * D...]
    dot_general x17 -> x6, matrix products: 61.1 us -> 24.1 us  [the longest x1 10.1 us: local(): jnp.dot(act, w_down[0], preferred_element_type=F32).astype(BF16)]
    scatter x1 -> x0, local copies, waits for them, and re-layouts: 34.5 us -> none  [local(): jnp.zeros((dropped, D), jnp.bfloat16).at[destination]]
    ppermute x7 -> x0, starting transfers between devices: 29 us -> none  [passed_along(): return lax.ppermute(block, axis, route)]
    convert_element_type x4 -> x0, local copies, waits for them, and re-layouts: 13.8 us -> none  [the longest x1 10.4 us: local(): picked.astype(jnp.float32)]
    gather x1 -> x0, local copies, waits for them, and re-layouts: 13.6 us -> none  [local(): picked = returned_rows[jnp.minimum(destination, dropped - 1)]]
  transfers between devices with their start and end apart: 9 -> 2, of which waited for: 8 -> 1; matrix products, arithmetic and copies ran while one was open for 28% -> 1% of each run, Pallas kernels for 0% -> 13%
where the time goes in v1:
time: 476 us; the launch traced here: 471 us
  blocking collectives  255 us (54%)
  Pallas kernels  60.2 us (13%)
  local copies, waits for them, and re-layouts  54.7 us (11%)
  waiting for transfers between devices  44.9 us (9%)
  matrix products  28.9 us (6%)
  between operations  14.3 us (3%)
  starting transfers between devices  10.8 us (2%)
    all_to_all x2, blocking collectives, exchange(): rows = lax.all_to_all(rows, 'exp', split_axis=1, concat_axis=1, tiled=True)  202 us
    pallas_call x1, Pallas kernels, mixer(): pl.pallas_call(mixer_kernel, out_shape=jax.ShapeDtypeStruct((T, HEADS * D...  60.2 us
    all_to_all x1, blocking collectives, exchange(): return lax.all_to_all(rows, 'ctx', split_axis=0, concat_axis=0, tiled=True)  52.8 us
    all_to_all x1, waiting for transfers between devices, exchange(): return lax.all_to_all(rows, 'ctx', split_axis=0, concat_axis=0, tiled=True)  44.1 us
    reshape x3, local copies, waits for them, and re-layouts, local(): returned = exchange(expert_out.reshape(n_ctx, n_exp, CAP, D)).reshape(-1, D)  18.4 us
    reshape x2, local copies, waits for them, and re-layouts, local(): outgoing = outgoing.reshape(n_ctx, n_exp, CAP, D)  11.5 us
    all_to_all x1, starting transfers between devices, exchange(): return lax.all_to_all(rows, 'ctx', split_axis=0, concat_axis=0, tiled=True)  10.8 us
    dot_general x1, matrix products, local(): jnp.dot(act, w_down[0], preferred_element_type=F32).astype(BF16)  10.1 us
  transfers between devices with their start and end apart: 2, of which 1 were waited for; matrix products, arithmetic and copies ran while one was open for 1% of the time, Pallas kernels for 13%

profile of v1, /device:TPU:5, one launch (start us, length us, event | category | flops | bytes accessed | tf_op | source)
XLA Modules:
  0.0 471.5 jit_solution(3011430941124958383)
XLA Ops:
  8.6 1.1 convert_reduce_fusion
  13.2 1.0 copy-done.3
  14.3 1.0 copy-done.4
  16.3 0.9 copy-done.6
  17.9 60.2 %mixer.1 = bf16[128,2048]{1,0:T(8,128)(2,1)S(1)} custom-call(bf16[128,1024]{1,0:T(8,128)(2,1)S(1)} %bitcast.56, bf16[128,1024]{1,0:T(8,128)(2,1)S(1)} %bitcast.57, bf16[128,2048]{1,0:T(8,128)(2,1)S(1)} %bitcast.54, bf16[128,2048]{1,0:T(8,128)(2,1)S(1)} %bitcast.55, f32[128,16]{1,0:T(8,128)S(1)} %copy.52.w_ref, f32[16,128]{1,0:T(8,128)S(1)} %bitcast.51, ...), custom_call_target="tpu_custom_call" | custom-call | flops 20000000000 | bytes 2000000 | tf_op jit(solution)/shard_map/mixer/pallas_call | solution.py:212
  78.2 4.8 %multiply_reduce_fusion.1 = (f32[128]{0:T(128)S(1)}, f32[128,2048]{1,0:T(8,128)S(1)}) fusion(bf16[128,2048]{1,0:T(8,128)(2,1)S(1)} %mixer.1, bf16[2048,2048]{1,0:T(8,128)(2,1)} %all-gather.2.cloned.1.call-done, bf16[1,128,2048]{2,1,0:T(8,128)(2,1)S(1)} %copy-done.11), kind=kOutput, calls=%fused_computation.17 | convolution fusion | flops 1074790272 | bytes 10486272 | tf_op jit(solution)/shard_map/dot_general | solution.py:239
  84.0 3.3 convolution_convert_fusion.1
  87.2 7.2 %reshape.122 = bf16[8,32,4,2048]{3,2,1,0:T(4,128)(2,1)} reshape(bf16[1024,2048]{1,0:T(8,128)(2,1)} %convolution_convert_fusion.1) | data formatting | bytes 8388608 | tf_op jit(solution)/shard_map/reshape | solution.py:259
  94.5 4.3 copy.57
  98.7 104.3 %all_to_all.20 = bf16[8,32,4,2048]{3,2,0,1:T(4,128)(2,1)S(1)} all-to-all(bf16[8,32,4,2048]{3,2,0,1:T(4,128)(2,1)S(1)} %copy.57), channel_id=1, replica_groups=mesh['ctx'=8,'exp'=32] {'exp'}, dimensions={1} | all-to-all | bytes 8388608 | tf_op jit(solution)/shard_map/all_to_all | solution.py:262
  203.1 2.9 copy.58
  206.0 52.8 %all_to_all.21 = bf16[8,32,4,2048]{3,2,1,0:T(4,128)(2,1)} all-to-all(bf16[8,32,4,2048]{3,2,1,0:T(4,128)(2,1)S(1)} %copy.58), channel_id=1, replica_groups=mesh['ctx'=8,'exp'=32] {'ctx'}, dimensions={0} | all-to-all | bytes 8388608 | tf_op jit(solution)/shard_map/all_to_all | solution.py:263
  258.7 6.9 %reshape.123 = bf16[1024,2048]{1,0:T(8,128)(2,1)} reshape(bf16[8,32,4,2048]{3,2,1,0:T(4,128)(2,1)} %all_to_all.21) | data formatting | bytes 8388608 | tf_op jit(solution)/shard_map/reshape | solution.py:265
  265.6 6.5 %fusion.2 = f32[1024,512]{1,0:T(8,128)} fusion(bf16[1024,2048]{1,0:T(8,128)(2,1)} %reshape.123, bf16[1,2048,512]{2,1,0:T(8,128)(2,1)} %param.30), kind=kOutput, calls=%fused_computation.6 | convolution fusion | flops 2147483648 | bytes 8388608 | tf_op jit(solution)/shard_map/dot_general | solution.py:267
  272.2 10.1 %convolution_convert_fusion = bf16[1024,2048]{1,0:T(8,128)(2,1)} fusion(bf16[1,512,2048]{2,1,0:T(8,128)(2,1)S(1)} %copy-done, f32[1024,512]{1,0:T(8,128)} %fusion.2, bf16[1024,2048]{1,0:T(8,128)(2,1)} %reshape.123, bf16[1,2048,512]{2,1,0:T(8,128)(2,1)} %param.29), kind=kOutput, calls=%fused_computation | convolution fusion | flops 4300210176 | bytes 14680064 | tf_op jit(solution)/shard_map/dot_general | solution.py:269
  282.3 7.2 %reshape.124 = bf16[8,32,4,2048]{3,2,1,0:T(4,128)(2,1)} reshape(bf16[1024,2048]{1,0:T(8,128)(2,1)} %convolution_convert_fusion) | data formatting | bytes 8388608 | tf_op jit(solution)/shard_map/reshape | solution.py:270
  289.5 4.3 copy.59
  293.7 97.4 %all_to_all.22 = bf16[8,32,4,2048]{3,2,0,1:T(4,128)(2,1)S(1)} all-to-all(bf16[8,32,4,2048]{3,2,0,1:T(4,128)(2,1)S(1)} %copy.59), channel_id=1, replica_groups=mesh['ctx'=8,'exp'=32] {'exp'}, dimensions={1} | all-to-all | bytes 8388608 | tf_op jit(solution)/shard_map/all_to_all | solution.py:262
  391.2 4.1 copy.60
  395.2 10.8 %all-to-all-start.3 = ((bf16[8,32,4,2048]{3,2,1,0:T(4,128)(2,1)}), bf16[8,32,4,2048]{3,2,1,0:T(4,128)(2,1)}, u32[]{:S(2)}, u32[]{:S(2)}) async-start(bf16[8,32,4,2048]{3,2,1,0:T(4,128)(2,1)} %copy.60), calls=%async_computation.3 | async-start | bytes 8388608 | tf_op jit(solution)/shard_map/all_to_all | solution.py:263
  408.0 44.1 %all-to-all-done.3 = bf16[8,32,4,2048]{3,2,1,0:T(4,128)(2,1)} async-done(((bf16[8,32,4,2048]{3,2,1,0:T(4,128)(2,1)}), bf16[8,32,4,2048]{3,2,1,0:T(4,128)(2,1)}, u32[]{:S(2)}, u32[]{:S(2)}) %all-to-all-start.3) | async-done | bytes 4194336 | tf_op jit(solution)/shard_map/all_to_all | solution.py:263
  452.1 6.9 %reshape.125 = bf16[1024,2048]{1,0:T(8,128)(2,1)} reshape(bf16[8,32,4,2048]{3,2,1,0:T(4,128)(2,1)} %all-to-all-done.3) | data formatting | bytes 8388608 | tf_op jit(solution)/shard_map/reshape | solution.py:270
  459.1 3.1 fusion.26
  463.7 1.0 fusion.11
  (52 shorter events, 11.0 us)
Async XLA Ops:
  6.5 265.6 %copy-start = (bf16[1,512,2048]{2,1,0:T(8,128)(2,1)S(1)}, bf16[1,512,2048]{2,1,0:T(8,128)(2,1)}, u32[]{:S(2)}) copy-start(bf16[1,512,2048]{2,1,0:T(8,128)(2,1)} %param.31) | copy-start | bytes 6291460
  6.5 71.6 %all-gather.2.cloned.1.call-start = ((), (), s32[]{:S(2)}) async-start(), calls=%async_computation.4 | async-start | bytes 9437184 | tf_op jit(solution)/shard_map/all_gather | solution.py:240
  11.8 0.7 copy-start.1
  12.5 0.7 copy-start.2
  13.2 1.0 copy-start.3
  14.3 1.0 copy-start.4
  15.3 0.9 copy-start.5
  16.3 0.9 copy-start.6
  17.2 0.7 copy-start.7
  17.9 60.3 %copy-start.11 = (bf16[1,128,2048]{2,1,0:T(8,128)(2,1)S(1)}, bf16[1,128,2048]{2,1,0:T(8,128)(2,1)}, u32[]{:S(2)}) copy-start(bf16[1,128,2048]{2,1,0:T(8,128)(2,1)} %param.24) | copy-start | bytes 1572868
  78.1 5.8 %copy-start.14 = (f32[2048]{0:T(1024)S(1)}, f32[2048]{0:T(1024)}, u32[]{:S(2)}) copy-start(f32[2048]{0:T(1024)} %param.26) | copy-start | bytes 24580
  83.0 1.0 copy-start.9
  395.2 10.8 %copy-start.12 = (f32[128,256]{1,0:T(8,128)S(1)}, f32[128,256]{1,0:T(8,128)}, u32[]{:S(2)}) copy-start(f32[128,256]{1,0:T(8,128)} %get-tuple-element.6) | copy-start | bytes 393220
  395.2 10.9 %copy-start.13 = (f32[2048]{0:T(1024)S(1)}, f32[2048]{0:T(1024)}, u32[]{:S(2)}) copy-start(f32[2048]{0:T(1024)} %param.33) | copy-start | bytes 24580
  395.2 56.9 %all-to-all-start.3 = ((bf16[8,32,4,2048]{3,2,1,0:T(4,128)(2,1)}), bf16[8,32,4,2048]{3,2,1,0:T(4,128)(2,1)}, u32[]{:S(2)}, u32[]{:S(2)}) async-start(bf16[8,32,4,2048]{3,2,1,0:T(4,128)(2,1)} %copy.60), calls=%async_computation.3 | async-start | bytes 8388608 | tf_op jit(solution)/shard_map/all_to_all | solution.py:263
  459.1 3.4 copy-start.8
  459.1 3.7 copy-start.10
  462.2 1.5 copy-start.15
Sparse Core Ops, SparseCore 0:
  9.2 64.5 all-gather.1

commit v2 on v1

--- a/solution.py
+++ b/solution.py
@@ -231,6 +231,263 @@
     )(queries, keys, values, out_gate, write_rate, write_rate.T, decay, decay.T, head_gain[None, :])
 
 
+PEERS = 32
+ROWS = 16
+HALF = T // 2
+GROUP = PEERS * ROWS
+AG_CHUNKS = (
+    ((1, 0), (1, 1), (2, 0), (2, 1), (3, 0), (3, 1), (4, 0)),
+    ((1, 1), (1, 0), (2, 1), (2, 0), (3, 1), (3, 0), (4, 1)),
+)
+RS_CHUNKS = (
+    ((4, 1), (3, 0), (3, 1), (2, 0), (2, 1), (1, 0), (1, 1)),
+    ((4, 0), (3, 1), (3, 0), (2, 1), (2, 0), (1, 1), (1, 0)),
+)
+BEHIND = {1: 1, 2: 3, 3: 5, 4: 7}
+AHEAD = {1: 2, 2: 4, 3: 6, 4: 7}
+OFFSETS = (0, -1, 1, -2, 2, -3, 3, 4)
+
+
+def moe_kernel(
+    x_ref, info_ref, wg_hbm, wu_hbm, wd_hbm, out_ref,
+    xg, stage, rows, outb, ret, rs_out, rs_in, y_ref, pick, high, low, wg, wu, wd,
+    w_sem, ag_send, ag_recv, in_send, in_recv, back_send, back_recv, rs_send, rs_recv,
+):
+    ctx = lax.axis_index("ctx")
+    exp = lax.axis_index("exp")
+    yy, zz = exp // 8, exp % 8
+    mine = ctx * 4 + yy
+    barrier = pltpu.get_barrier_semaphore()
+
+    def peer(k):
+        c, y = (ctx + k // 4) % 8, (yy + k % 4) % 4
+        return c * 4 + y, {"ctx": c, "exp": y * 8 + zz}
+
+    def along(step):
+        return {"ctx": ctx, "exp": yy * 8 + (zz + step + 8) % 8}
+
+    weights = [
+        pltpu.make_async_copy(s, d, w_sem.at[i])
+        for i, (s, d) in enumerate(((wg_hbm, wg), (wu_hbm, wu), (wd_hbm, wd)))
+    ]
+    for copy in weights:
+        copy.start()
+
+    def greet(k, carry):
+        pl.semaphore_signal(barrier, inc=1, device_id=peer(k)[1], device_id_type=MESH)
+        return carry
+
+    for step in (1, -1):
+        pl.semaphore_signal(barrier, inc=1, device_id=along(step), device_id_type=MESH)
+    lax.fori_loop(1, PEERS, greet, 0)
+    xg[0] = x_ref[...]
+    pl.semaphore_wait(barrier, PEERS + 1)
+
+    def half(h):
+        return pl.ds(h * HALF, HALF)
+
+    def gather(way, i):
+        d, h = AG_CHUNKS[way][i]
+        slot = (BEHIND, AHEAD)[way]
+        src = x_ref.at[half(h)] if d == 1 else xg.at[slot[d - 1], half(h)]
+        return pltpu.make_async_remote_copy(
+            src_ref=src,
+            dst_ref=xg.at[slot[d], half(h)],
+            send_sem=ag_send.at[way, i],
+            recv_sem=ag_recv.at[way, i],
+            device_id=along((1, -1)[way]),
+            device_id_type=MESH,
+        )
+
+    def pass_on(first, end):
+        for i in range(first, end):
+            for way in (0, 1):
+                gather(way, i).wait_recv()
+                if i + 2 < 7:
+                    gather(way, i + 2).start()
+
+    for i in (0, 1):
+        for way in (0, 1):
+            gather(way, i).start()
+
+    row = lax.broadcasted_iota(jnp.int32, (GROUP, T), 0)
+    slot_of = (row % CAP).astype(F32)
+    spread = (
+        lax.broadcasted_iota(jnp.int32, (GROUP, PEERS), 0) // ROWS
+        == lax.broadcasted_iota(jnp.int32, (GROUP, PEERS), 1)
+    )
+    spread_b, spread_f = spread.astype(F32).astype(BF16), spread.astype(F32)
+    earlier = (
+        lax.broadcasted_iota(jnp.int32, (T, T), 0) < lax.broadcasted_iota(jnp.int32, (T, T), 1)
+    ).astype(F32).astype(BF16)
+    named = (lax.broadcasted_iota(jnp.int32, (PEERS, T), 0) * 8 + zz).astype(F32)
+
+    def tables(g):
+        for s in range(4):
+            info = info_ref[(zz + OFFSETS[g * 4 + s] + 8) % 8]
+            member = jnp.zeros((PEERS, T), F32)
+            weight = jnp.zeros((PEERS, T), F32)
+            for j in range(TOP):
+                hit = info[j : j + 1] == named
+                member = member + jnp.where(hit, 1.0, 0.0)
+                weight = weight + jnp.where(hit, info[TOP + j : TOP + j + 1], 0.0)
+            member_b = member.astype(BF16)
+            before = jnp.dot(member_b, earlier, preferred_element_type=F32)
+            here = jnp.dot(spread_b, member_b, preferred_element_type=F32)
+            place = jnp.dot(spread_b, before.astype(BF16), preferred_element_type=F32)
+            share = jnp.dot(spread_f, weight, precision=HIGHEST, preferred_element_type=F32)
+            taken = (here > 0.5) & (place == slot_of) & (row // CAP % 4 == s)
+            at = pl.ds(s * T, T)
+            pick[g, :, at] = jnp.where(taken, 1.0, 0.0).astype(BF16)
+            scaled = jnp.where(taken, share, 0.0).T
+            top = scaled.astype(BF16)
+            high[g, at, :] = top
+            low[g, at, :] = (scaled - top.astype(F32)).astype(BF16)
+
+    def tiles(body):
+        def run(i, carry):
+            body(pl.ds(pl.multiple_of(i * 512, 512), 512))
+            return carry
+
+        lax.fori_loop(0, D // 512, run, 0)
+
+    def own(p):
+        return pl.ds(pl.multiple_of(p * ROWS, ROWS), ROWS)
+
+    def exchange(src, dst, send, recv, g):
+        def go(k, carry):
+            p, device = peer(k)
+            pltpu.make_async_remote_copy(
+                src_ref=src.at[g, own(p)],
+                dst_ref=dst.at[g, own(mine)],
+                send_sem=send.at[g],
+                recv_sem=recv.at[g],
+                device_id=device,
+                device_id_type=MESH,
+            ).start()
+            return carry
+
+        lax.fori_loop(1, PEERS, go, 0)
+        dst[g, own(mine)] = src[g, own(mine)]
+
+    def all_of(ref, sem, g):
+        some = ref.at[g, pl.ds(0, GROUP - ROWS)]
+        return pltpu.make_async_copy(some, some, sem.at[g])
+
+    def dispatch(g):
+        def tile(at):
+            x = xg[g * 4 : g * 4 + 4, :, at].reshape(GROUP, 512)
+            stage[g, :, at] = jnp.dot(pick[g], x, preferred_element_type=F32).astype(BF16)
+
+        tiles(tile)
+        exchange(stage, rows, in_send, in_recv, g)
+
+    def experts(g):
+        all_of(rows, in_recv, g).wait()
+
+        def tile(i, carry):
+            at = pl.ds(pl.multiple_of(i * 256, 256), 256)
+            x = rows[g, at, :]
+            gate = jnp.dot(x, wg[...], preferred_element_type=F32)
+            up = jnp.dot(x, wu[...], preferred_element_type=F32)
+            act = (gate / (1.0 + jnp.exp(-gate)) * up).astype(BF16)
+            outb[g, at, :] = jnp.dot(act, wd[...], preferred_element_type=F32).astype(BF16)
+            return carry
+
+        lax.fori_loop(0, GROUP // 256, tile, 0)
+        exchange(outb, ret, back_send, back_recv, g)
+
+    def combine(g):
+        all_of(ret, back_recv, g).wait()
+
+        def tile(at):
+            r = ret[g, :, at]
+            total = jnp.dot(high[g], r, preferred_element_type=F32) + jnp.dot(
+                low[g], r, preferred_element_type=F32
+            )
+            y_ref[g * 4 : g * 4 + 4, :, at] = total.reshape(4, T, 512)
+
+        tiles(tile)
+
+    tables(0)
+    pass_on(0, 2)
+    tables(1)
+    pass_on(2, 4)
+    dispatch(0)
+    pass_on(4, 7)
+    dispatch(1)
+    for copy in weights:
+        copy.wait()
+    experts(0)
+    experts(1)
+    combine(0)
+    combine(1)
+
+    def reduce(way, i):
+        return pltpu.make_async_remote_copy(
+            src_ref=rs_out.at[way, i],
+            dst_ref=rs_in.at[way, i],
+            send_sem=rs_send.at[way, i],
+            recv_sem=rs_recv.at[way, i],
+            device_id=along((1, -1)[way]),
+            device_id_type=MESH,
+        )
+
+    for i in range(7):
+        for way in (0, 1):
+            d, h = RS_CHUNKS[way][i]
+            part = y_ref[(AHEAD, BEHIND)[way][d], half(h)]
+            if i >= 2:
+                reduce(way, i - 2).wait_recv()
+                part = part + rs_in[way, i - 2].astype(F32)
+            rs_out[way, i] = part.astype(BF16)
+            reduce(way, i).start()
+    for i in (5, 6):
+        for way in (0, 1):
+            reduce(way, i).wait_recv()
+    for h in (0, 1):
+        total = y_ref[0, half(h)]
+        for way in (0, 1):
+            total = total + rs_in[way, RS_CHUNKS[way].index((1, h))].astype(F32)
+        out_ref[half(h)] = total
+
+    for i in range(7):
+        for way in (0, 1):
+            gather(way, i).wait_send()
+            reduce(way, i).wait_send()
+    for g in (0, 1):
+        all_of(stage, in_send, g).wait()
+        all_of(outb, back_send, g).wait()
+
+
+def moe(x, info, w_gate, w_up, w_down):
+    group = pltpu.VMEM((2, GROUP, D), BF16)
+    table = pltpu.VMEM((2, GROUP, GROUP), BF16)
+    ring = pltpu.VMEM((2, 7, HALF, D), BF16)
+    dma = pltpu.SemaphoreType.DMA
+    vmem, anywhere = pl.BlockSpec(memory_space=pltpu.VMEM), pl.BlockSpec(memory_space=pl.ANY)
+    return pl.pallas_call(
+        moe_kernel,
+        out_shape=jax.ShapeDtypeStruct((T, D), F32),
+        in_specs=[vmem, vmem, anywhere, anywhere, anywhere],
+        out_specs=vmem,
+        scratch_shapes=[
+            pltpu.VMEM((8, T, D), BF16),
+            group, group, group, group, ring, ring,
+            pltpu.VMEM((8, T, D), F32),
+            table, table, table,
+            pltpu.VMEM((D, 512), BF16), pltpu.VMEM((D, 512), BF16), pltpu.VMEM((512, D), BF16),
+            dma((3,)), dma((2, 7)), dma((2, 7)), dma((2,)), dma((2,)), dma((2,)), dma((2,)),
+            dma((2, 7)), dma((2, 7)),
+        ],
+        compiler_params=pltpu.CompilerParams(
+            collective_id=1, has_side_effects=True, vmem_limit_bytes=62 * 2**20
+        ),
+        cost_estimate=pl.CostEstimate(flops=12 * 10**9, bytes_accessed=10**7, transcendentals=0),
+        name="moe",
+    )(x, info, w_gate, w_up, w_down)
+
+
 def local(
     queries, keys, values, out_gate, write_rate, decay, head_gain, residual, out_proj, ffn_gain,
     expert_ids, route_weight, w_gate, w_up, w_down, ablate_mask, direction,
@@ -243,36 +500,10 @@
     ffn_in = (
         hidden_sum / jnp.sqrt(jnp.mean(hidden_sum * hidden_sum, -1, keepdims=True) + 1e-06) * ffn_gain
     ).astype(BF16)
-    n_ctx, n_exp = lax.axis_size("ctx"), lax.axis_size("exp")
-    window = n_ctx * n_exp
-    ids = expert_ids[0]
-    named = ids[:, :, None] == jnp.arange(window, dtype=jnp.int32)[None, None, :]
-    member = jnp.sum(named.astype(F32), axis=1)
-    weight = jnp.sum(jnp.where(named, route_weight[0][:, :, None], 0.0), axis=1)
-    earlier = jnp.tril(jnp.ones((T, T), F32), -1)
-    slot = jnp.dot(earlier, member, preferred_element_type=F32)
-    slots = jnp.arange(CAP, dtype=F32)
-    taken = (slot[:, :, None] == slots) & (member[:, :, None] > 0)
-    pick = taken.astype(BF16).reshape(T, window * CAP)
-    weights = jnp.where(taken, weight[:, :, None], 0.0).reshape(T, window * CAP)
-    outgoing = jnp.dot(pick.T, ffn_in, preferred_element_type=F32).astype(BF16)
-    outgoing = outgoing.reshape(n_ctx, n_exp, CAP, D)
-
-    def exchange(rows):
-        rows = lax.all_to_all(rows, "exp", split_axis=1, concat_axis=1, tiled=True)
-        return lax.all_to_all(rows, "ctx", split_axis=0, concat_axis=0, tiled=True)
-
-    rows = exchange(outgoing).reshape(-1, D)
-    gate_part = jnp.dot(rows, w_gate[0], preferred_element_type=F32)
-    up_part = jnp.dot(rows, w_up[0], preferred_element_type=F32)
-    act = (jax.nn.silu(gate_part) * up_part).astype(BF16)
-    expert_out = jnp.dot(act, w_down[0], preferred_element_type=F32).astype(BF16)
-    returned = exchange(expert_out.reshape(n_ctx, n_exp, CAP, D)).reshape(-1, D)
-    high = weights.astype(BF16)
-    rest = (weights - high.astype(F32)).astype(BF16)
-    moe_sum = jnp.dot(high, returned, preferred_element_type=F32) + jnp.dot(
-        rest, returned, preferred_element_type=F32
-    )
+    listed = jnp.concatenate([expert_ids[0].T.astype(F32), route_weight[0].T], axis=0)
+    columns = [[y * 8 + z for z in range(8)] for y in range(4)]
+    info = lax.all_gather(listed, "exp", axis_index_groups=columns)
+    moe_sum = moe(ffn_in, info, w_gate[0], w_up[0], w_down[0])
     combined = hidden_sum + moe_sum
     unit_dir = direction / jnp.sqrt(jnp.sum(direction * direction) + 1e-06)
     along = jnp.sum(combined * unit_dir[None, :], axis=1)

time: 476 us -> 278 us (0.58)
  blocking collectives: 255 us -> 24.2 us
  Pallas kernels: 60.2 us -> 219 us
  local copies, waits for them, and re-layouts: 54.7 us -> 8.35 us
  waiting for transfers between devices: 44.9 us -> 0.73 us
  matrix products: 28.9 us -> 4.77 us
  starting transfers between devices: 10.8 us -> 0.01 us
    all_to_all x3 -> x0, blocking collectives: 255 us -> none  [the longest x2 202 us: exchange(): rows = lax.all_to_all(rows, 'exp', split_axis=1, concat_axis=1, tiled=True)]
    pallas_call x0 -> x1, Pallas kernels: none -> 177 us  [moe(): pl.pallas_call(moe_kernel, out_shape=jax.ShapeDtypeStruct((T, D), F32), i...]
    all_to_all x1 -> x0, waiting for transfers between devices: 44.1 us -> none  [exchange(): return lax.all_to_all(rows, 'ctx', split_axis=0, concat_axis=0, tiled=True)]
    reshape x6 -> x0, local copies, waits for them, and re-layouts: 36.8 us -> none  [the longest x3 18.4 us: local(): returned = exchange(expert_out.reshape(n_ctx, n_exp, CAP, D)).reshape(-1, D)]
    all_gather x0 -> x1, blocking collectives: none -> 24.2 us  [local(): info = lax.all_gather(listed, 'exp', axis_index_groups=columns)]
    dot_general x6 -> x0, matrix products: 24.1 us -> none  [the longest x1 10.1 us: local(): jnp.dot(act, w_down[0], preferred_element_type=F32).astype(BF16)]
    pallas_call x1, Pallas kernels: 60.2 us -> 41.4 us  [mixer(): pl.pallas_call(mixer_kernel, out_shape=jax.ShapeDtypeStruct((T, HEADS * D...]
    all_to_all x1 -> x0, starting transfers between devices: 10.8 us -> none  [exchange(): return lax.all_to_all(rows, 'ctx', split_axis=0, concat_axis=0, tiled=True)]
  transfers between devices with their start and end apart: 2 -> 1, of which waited for: 1 -> 0; matrix products, arithmetic and copies ran while one was open for 1% -> 2% of each run, Pallas kernels for 13% -> 15%
where the time goes in v2:
time: 278 us; the launch traced here: 277 us
  Pallas kernels  219 us (79%)
  blocking collectives  24.2 us (9%)
  between operations  14.2 us (5%)
  local copies, waits for them, and re-layouts  8.35 us (3%)
  other arithmetic  6.08 us (2%)
  matrix products  4.77 us (2%)
    pallas_call x1, Pallas kernels, moe(): pl.pallas_call(moe_kernel, out_shape=jax.ShapeDtypeStruct((T, D), F32), i...  177 us
    pallas_call x1, Pallas kernels, mixer(): pl.pallas_call(mixer_kernel, out_shape=jax.ShapeDtypeStruct((T, HEADS * D...  41.4 us
    all_gather x1, blocking collectives, local(): info = lax.all_gather(listed, 'exp', axis_index_groups=columns)  24.2 us
    unnamed x21, local copies, waits for them, and re-layouts  6.76 us
  transfers between devices with their start and end apart: 1, of which 0 were waited for; matrix products, arithmetic and copies ran while one was open for 2% of the time, Pallas kernels for 15%

profile of v2, /device:TPU:5, one launch (start us, length us, event | category | flops | bytes accessed | tf_op | source)
XLA Modules:
  0.0 277.0 jit_solution(11130467365017589166)
XLA Ops:
  6.5 0.7 all-gather.4.cloned.1.call-update
  7.3 0.8 copy.21.w_ref
  8.1 0.8 copy.22.d_ref
  8.9 0.7 copy.29
  9.5 1.3 multiply_reduce_fusion.2
  11.5 0.7 fusion.1
  12.2 24.2 %all-gather.1.info_ref = f32[8,20,128]{2,1,0:T(8,128)} all-gather(f32[1,20,128]{2,1,0:T(8,128)S(1)} %maximum_bitcast_fusion), channel_id=2, replica_groups={{0,1,2,3,4,5,6,7},{8,9,10,11,12,13,14,15},{16,17,18,19,20,21,22,23},{24..., dimensions={0}, use_global_device_ids=true | all-gather | bytes 92160 | tf_op jit(solution)/shard_map/all_gather | solution.py:505
  36.4 0.7 broadcast_divide_fusion
  37.1 0.7 copy-done
  37.8 0.7 copy-done.1
  38.5 1.0 copy-done.2
  39.6 1.0 copy-done.3
  40.6 0.9 copy-done.4
  41.6 1.0 copy-done.5
  42.5 0.7 copy-done.6
  43.2 41.4 %mixer.1 = bf16[128,2048]{1,0:T(8,128)(2,1)S(1)} custom-call(bf16[128,1024]{1,0:T(8,128)(2,1)S(1)} %bitcast.40, bf16[128,1024]{1,0:T(8,128)(2,1)S(1)} %bitcast.41, bf16[128,2048]{1,0:T(8,128)(2,1)S(1)} %bitcast.38, bf16[128,2048]{1,0:T(8,128)(2,1)S(1)} %bitcast.39, f32[128,16]{1,0:T(8,128)S(1)} %copy.21.w_ref, f32[16,128]{1,0:T(8,128)S(1)} %bitcast.35, ...), custom_call_target="tpu_custom_call" | custom-call | flops 20000000000 | bytes 2000000 | tf_op jit(solution)/shard_map/mixer/pallas_call | solution.py:212
  84.5 0.0 copy-start.8
  84.5 0.0 all-gather.4.cloned.1.call-done
  84.6 0.0 copy-done.7
  84.6 4.8 %multiply_reduce_fusion.1 = (f32[128]{0:T(128)S(1)}, f32[128,2048]{1,0:T(8,128)S(1)}) fusion(bf16[128,2048]{1,0:T(8,128)(2,1)S(1)} %mixer.1, bf16[2048,2048]{1,0:T(8,128)(2,1)} %all-gather.4.cloned.1.call-done, bf16[1,128,2048]{2,1,0:T(8,128)(2,1)S(1)} %copy-done.7), kind=kOutput, calls=%fused_computation.4 | convolution fusion | flops 1074790272 | bytes 10486272 | tf_op jit(solution)/shard_map/dot_general | solution.py:496
  89.4 1.0 multiply_convert_fusion.x_ref
  90.4 177.4 %moe.1 = f32[128,2048]{1,0:T(8,128)} custom-call(bf16[128,2048]{1,0:T(8,128)(2,1)} %multiply_convert_fusion.x_ref, f32[8,20,128]{2,1,0:T(8,128)} %all-gather.1.info_ref, bf16[2048,512]{1,0:T(8,128)(2,1)} %bitcast.44, bf16[2048,512]{1,0:T(8,128)(2,1)} %bitcast.45, bf16[512,2048]{1,0:T(8,128)(2,1)} %bitcast.46), custom_call_target="tpu_custom_call" | custom-call | flops 12000000000 | bytes 10000000 | tf_op jit(solution)/shard_map/moe/pallas_call | solution.py:469
  267.8 1.4 multiply_reduce_fusion
  269.2 1.0 fusion
  (15 shorter events, 0.0 us)
Async XLA Ops:
  6.5 78.0 %all-gather.4.cloned.1.call-start = ((), (), s32[]{:S(2)}) async-start(), calls=%async_computation | async-start | bytes 9437184 | tf_op jit(solution)/shard_map/all_gather | solution.py:497
  37.1 0.7 copy-start
  37.8 0.7 copy-start.1
  38.5 1.0 copy-start.2
  39.6 1.1 copy-start.3
  40.6 1.0 copy-start.4
  41.6 1.0 copy-start.5
  42.5 0.7 copy-start.6
  43.2 41.4 %copy-start.7 = (bf16[1,128,2048]{2,1,0:T(8,128)(2,1)S(1)}, bf16[1,128,2048]{2,1,0:T(8,128)(2,1)}, u32[]{:S(2)}) copy-start(bf16[1,128,2048]{2,1,0:T(8,128)(2,1)} %param.24) | copy-start | bytes 1572868
  84.5 4.8 %copy-start.8 = (f32[2048]{0:T(1024)S(1)}, f32[2048]{0:T(1024)}, u32[]{:S(2)}) copy-start(f32[2048]{0:T(1024)} %param.26) | copy-start | bytes 24580
  90.4 178.8 %copy-start.9 = (s32[1,128]{1,0:T(1,128)S(1)}, s32[1,128]{1,0:T(1,128)}, u32[]{:S(2)}) copy-start(s32[1,128]{1,0:T(1,128)} %param.32) | copy-start | bytes 1540
Sparse Core Ops, SparseCore 0:
  9.2 54.4 all-gather.3

commit v3 on v2

--- a/solution.py
+++ b/solution.py
@@ -47,20 +47,59 @@
 
 
 def mixer_kernel(
-    q_ref, k_ref, v_ref, gate_ref, w_ref, wt_ref, d_ref, dt_ref, gain_ref, out_ref,
-    lc_ref, lr_ref, loc_ref, qeff_ref, car_ref, off_ref, got_ref, sent_ref, send_sem, recv_sem,
+    q_ref, k_ref, v_ref, gate_ref, w_ref, wt_ref, d_ref, dt_ref, gain_ref,
+    res_ref, proj_ref, norm_ref, info_ref, hidden_ref, x_ref, infos_ref,
+    lc_ref, lr_ref, loc_ref, qeff_ref, car_ref, off_ref, got_ref, sent_ref, out_ref, wo, infos,
+    send_sem, recv_sem, wo_send, wo_recv, info_send, info_recv,
 ):
     me = lax.axis_index("ctx")
+    exp = lax.axis_index("exp")
+    yy, zz = exp // 8, exp % 8
     last = N_CTX - 1
     barrier = pltpu.get_barrier_semaphore()
 
+    def column_peer(k):
+        return {"ctx": me, "exp": yy * 8 + (zz + k) % 8}
+
+    def chain_peer(step):
+        return {"ctx": (me + step + 8) % 8, "exp": exp}
+
     @pl.when(me > 0)
     def _():
-        pl.semaphore_signal(barrier, inc=1, device_id={"ctx": me - 1}, device_id_type=MESH)
+        pl.semaphore_signal(barrier, inc=1, device_id=chain_peer(-1), device_id_type=MESH)
 
     @pl.when(me < last)
     def _():
-        pl.semaphore_signal(barrier, inc=1, device_id={"ctx": me + 1}, device_id_type=MESH)
+        pl.semaphore_signal(barrier, inc=1, device_id=chain_peer(1), device_id_type=MESH)
+
+    for step in (2, -2):
+        pl.semaphore_signal(barrier, inc=1, device_id=chain_peer(step), device_id_type=MESH)
+    for k in range(1, 8):
+        pl.semaphore_signal(barrier, inc=1, device_id=column_peer(k), device_id_type=MESH)
+
+    left, right, opposite = (me + 6) % 8, (me + 2) % 8, (me + 4) % 8
+    partner = {"ctx": me + 1 - 2 * (me % 2), "exp": exp}
+    routes = (
+        (None, me, 0, chain_peer(2)), (None, me, 1, chain_peer(2)),
+        (None, me, 0, chain_peer(-2)), (None, me, 1, chain_peer(-2)),
+        (None, me, 0, partner), (None, me, 1, partner),
+        (left, left, 0, chain_peer(2)), (right, right, 1, chain_peer(-2)),
+        (left, left, 0, partner), (left, left, 1, partner),
+        (right, right, 0, partner), (right, right, 1, partner),
+        (opposite, opposite, 0, partner), (opposite, opposite, 1, partner),
+    )
+
+    def shard(n):
+        held, index, h, device = routes[n]
+        at = pl.ds(h * 128, 128)
+        return pltpu.make_async_remote_copy(
+            src_ref=proj_ref.at[at] if held is None else wo.at[held, at],
+            dst_ref=wo.at[index, at],
+            send_sem=wo_send.at[n],
+            recv_sem=wo_recv.at[n],
+            device_id=device,
+            device_id_type=MESH,
+        )
 
     rows = lax.broadcasted_iota(jnp.int32, (T, T), 0)
     cols = lax.broadcasted_iota(jnp.int32, (T, T), 1)
@@ -71,6 +110,28 @@
     lr_ref[...] = jnp.dot(jnp.log(dt_ref[...]), upper, precision=HIGHEST, preferred_element_type=F32)
     ones = jnp.ones((8, DK), F32)
     head_lane = lax.broadcasted_iota(jnp.int32, (T, HEADS), 1)
+
+    @pl.when((me > 0) & (me < last))
+    def _():
+        pl.semaphore_wait(barrier, 11)
+
+    @pl.when((me == 0) | (me == last))
+    def _():
+        pl.semaphore_wait(barrier, 10)
+
+    for k in range(1, 8):
+        pltpu.make_async_remote_copy(
+            src_ref=info_ref,
+            dst_ref=infos.at[zz],
+            send_sem=info_send,
+            recv_sem=info_recv,
+            device_id=column_peer(k),
+            device_id_type=MESH,
+        ).start()
+    for n in (0, 3, 1, 2, 4, 5):
+        shard(n).start()
+    infos[zz] = info_ref[...]
+    wo[me] = proj_ref[...]
     in_16 = (rows // 16 == cols // 16) & (rows > cols)
 
     def column(array, h):
@@ -140,13 +201,10 @@
 
     lax.fori_loop(0, KH // 2, maps, 0)
 
-    @pl.when((me > 0) & (me < last))
-    def _():
-        pl.semaphore_wait(barrier, 2)
-
-    @pl.when((me == 0) | (me == last))
-    def _():
-        pl.semaphore_wait(barrier, 1)
+    shard(0).wait_recv()
+    shard(6).start()
+    shard(3).wait_recv()
+    shard(7).start()
 
     def hop(h):
         return pltpu.make_async_remote_copy(
@@ -154,7 +212,7 @@
             dst_ref=got_ref.at[h],
             send_sem=send_sem.at[h],
             recv_sem=recv_sem.at[h],
-            device_id={"ctx": jnp.minimum(me + 1, last)},
+            device_id={"ctx": jnp.minimum(me + 1, last), "exp": exp},
             device_id_type=MESH,
         )
 
@@ -182,6 +240,13 @@
 
         lax.fori_loop(0, HEADS, relay, 0)
 
+    shard(8).start()
+    shard(11).start()
+    for n in (1, 2):
+        shard(n).wait_recv()
+    shard(9).start()
+    shard(10).start()
+
     gain = gain_ref[...]
 
     def finish(h, carry):
@@ -198,6 +263,31 @@
 
     lax.fori_loop(0, HEADS, finish, 0)
 
+    for n in (6, 7):
+        shard(n).wait_recv()
+        shard(n + 6).start()
+    for n in (4, 5, 8, 9, 10, 11, 12, 13):
+        shard(n).wait_recv()
+
+    def project(i, total):
+        at = pl.ds(pl.multiple_of(i * 512, 512), 512)
+        part = res_ref[:, at].astype(F32)
+        for j in range(8):
+            part = part + jnp.dot(
+                out_ref[:, j * 256 : j * 256 + 256], wo[j, :, at], preferred_element_type=F32
+            )
+        hidden_ref[:, at] = part
+        return total + jnp.sum(part * part, axis=1, keepdims=True)
+
+    total = lax.fori_loop(0, D // 512, project, jnp.zeros((T, 1), F32))
+    x_ref[...] = (hidden_ref[...] * lax.rsqrt(total / D + 1e-06) * norm_ref[...]).astype(BF16)
+    seven = infos.at[pl.ds(0, 7)]
+    pltpu.make_async_copy(seven, seven, info_recv).wait()
+    pltpu.make_async_copy(seven, seven, info_send).wait()
+    infos_ref[...] = infos[...]
+    for n in range(14):
+        shard(n).wait_send()
+
     @pl.when(me < last)
     def _():
         def drain(h, carry):
@@ -207,28 +297,44 @@
         lax.fori_loop(0, HEADS, drain, 0)
 
 
-def mixer(queries, keys, values, out_gate, write_rate, decay, head_gain):
+def mixer(
+    queries, keys, values, out_gate, write_rate, decay, head_gain, residual, out_proj, ffn_gain, listed
+):
     square = pltpu.VMEM((HEADS, DK, DV), F32)
     return pl.pallas_call(
         mixer_kernel,
-        out_shape=jax.ShapeDtypeStruct((T, HEADS * DV), BF16),
-        in_specs=[pl.BlockSpec(memory_space=pltpu.VMEM)] * 9,
-        out_specs=pl.BlockSpec(memory_space=pltpu.VMEM),
+        out_shape=[
+            jax.ShapeDtypeStruct((T, D), F32),
+            jax.ShapeDtypeStruct((T, D), BF16),
+            jax.ShapeDtypeStruct((8, 24, T), F32),
+        ],
+        in_specs=[pl.BlockSpec(memory_space=pltpu.VMEM)] * 13,
+        out_specs=[pl.BlockSpec(memory_space=pltpu.VMEM)] * 3,
         scratch_shapes=[
             pltpu.VMEM((T, HEADS), F32),
             pltpu.VMEM((HEADS, T), F32),
             square, square, square, square,
             pltpu.VMEM((HEADS, DK, DV), STATE),
             pltpu.VMEM((HEADS, DK, DV), STATE),
+            pltpu.VMEM((T, HEADS * DV), BF16),
+            pltpu.VMEM((N_CTX, 256, D), BF16),
+            pltpu.VMEM((8, 24, T), F32),
             pltpu.SemaphoreType.DMA((HEADS,)),
             pltpu.SemaphoreType.DMA((HEADS,)),
+            pltpu.SemaphoreType.DMA((14,)),
+            pltpu.SemaphoreType.DMA((14,)),
+            pltpu.SemaphoreType.DMA,
+            pltpu.SemaphoreType.DMA,
         ],
         compiler_params=pltpu.CompilerParams(
             collective_id=0, has_side_effects=True, vmem_limit_bytes=40 * 2**20
         ),
         cost_estimate=pl.CostEstimate(flops=20 * 10**9, bytes_accessed=2 * 10**6, transcendentals=0),
         name="mixer",
-    )(queries, keys, values, out_gate, write_rate, write_rate.T, decay, decay.T, head_gain[None, :])
+    )(
+        queries, keys, values, out_gate, write_rate, write_rate.T, decay, decay.T, head_gain[None, :],
+        residual, out_proj, ffn_gain[None, :], listed,
+    )
 
 
 PEERS = 32
@@ -492,17 +598,13 @@
     queries, keys, values, out_gate, write_rate, decay, head_gain, residual, out_proj, ffn_gain,
     expert_ids, route_weight, w_gate, w_up, w_down, ablate_mask, direction,
 ):
-    mixed = mixer(queries[0], keys[0], values[0], out_gate[0], write_rate[0], decay[0], head_gain)
-    projected = jnp.dot(
-        mixed, lax.all_gather(out_proj, "ctx", axis=0, tiled=True), preferred_element_type=F32
+    listed = jnp.concatenate(
+        [expert_ids[0].T.astype(F32), route_weight[0].T, jnp.zeros((4, T), F32)], axis=0
     )
-    hidden_sum = residual[0].astype(F32) + projected
-    ffn_in = (
-        hidden_sum / jnp.sqrt(jnp.mean(hidden_sum * hidden_sum, -1, keepdims=True) + 1e-06) * ffn_gain
-    ).astype(BF16)
-    listed = jnp.concatenate([expert_ids[0].T.astype(F32), route_weight[0].T], axis=0)
-    columns = [[y * 8 + z for z in range(8)] for y in range(4)]
-    info = lax.all_gather(listed, "exp", axis_index_groups=columns)
+    hidden_sum, ffn_in, info = mixer(
+        queries[0], keys[0], values[0], out_gate[0], write_rate[0], decay[0], head_gain, residual[0],
+        out_proj, ffn_gain, listed,
+    )
     moe_sum = moe(ffn_in, info, w_gate[0], w_up[0], w_down[0])
     combined = hidden_sum + moe_sum
     unit_dir = direction / jnp.sqrt(jnp.sum(direction * direction) + 1e-06)

time: 278 us -> 266 us (0.957)
  Pallas kernels: 219 us -> 248 us
  blocking collectives: 24.2 us -> 0 us
  between operations: 14.2 us -> 0.77 us
  matrix products: 4.77 us -> 0 us
  local copies, waits for them, and re-layouts: 8.35 us -> 12.8 us
    pallas_call x1, Pallas kernels: 41.4 us -> 67.2 us  [mixer(): pl.pallas_call(mixer_kernel, out_shape=[jax.ShapeDtypeStruct((T, D), F32)...]
    all_gather x1 -> x0, blocking collectives: 24.2 us -> none  [local(): info = lax.all_gather(listed, 'exp', axis_index_groups=columns)]
    dot_general x1 -> x0, matrix products: 4.77 us -> none  [local(): jnp.dot(mixed, lax.all_gather(out_proj, 'ctx', axis=0, tiled=True), prefe...]
    unnamed x21 -> x29, local copies, waits for them, and re-layouts: 6.76 us -> 11.1 us
    pallas_call x1, Pallas kernels: 177 us -> 181 us  [moe(): pl.pallas_call(moe_kernel, out_shape=jax.ShapeDtypeStruct((T, D), F32), i...]
  transfers between devices with their start and end apart: 1 -> 0, of which waited for: 0 -> 0; matrix products, arithmetic and copies ran while one was open for 2% -> 0% of each run, Pallas kernels for 15% -> 0%
where the time goes in v3:
time: 266 us; the launch traced here: 265 us
  Pallas kernels  248 us (93%)
  local copies, waits for them, and re-layouts  12.8 us (5%)
  other arithmetic  3.77 us (1%)
    pallas_call x1, Pallas kernels, moe(): pl.pallas_call(moe_kernel, out_shape=jax.ShapeDtypeStruct((T, D), F32), i...  181 us
    pallas_call x1, Pallas kernels, mixer(): pl.pallas_call(mixer_kernel, out_shape=[jax.ShapeDtypeStruct((T, D), F32)...  67.2 us
    unnamed x29, local copies, waits for them, and re-layouts  11.1 us

profile of v3, /device:TPU:5, one launch (start us, length us, event | category | flops | bytes accessed | tf_op | source)
XLA Modules:
  0.0 265.2 jit_solution(16939684338875655118)
XLA Ops:
  0.0 0.8 copy.19.w_ref
  0.8 0.8 copy.20.d_ref
  1.6 0.7 copy.26
  2.3 0.7 fusion.1
  3.0 0.1 pad.2.clone
  3.1 0.1 maximum_maximum_fusion.info_ref
  3.1 0.7 copy-done
  3.8 0.7 copy-done.1
  4.5 1.2 copy-done.2
  5.8 1.0 copy-done.3
  6.8 1.0 copy-done.4
  7.8 1.0 copy-done.5
  8.9 0.9 copy-done.6
  9.8 0.9 copy-done.7
  10.8 0.7 copy-done.8
  11.5 0.7 copy-done.9
  12.1 67.2 %mixer.1 = (f32[128,2048]{1,0:T(8,128)S(1)}, bf16[128,2048]{1,0:T(8,128)(2,1)S(1)}, f32[8,24,128]{2,1,0:T(8,128)S(1)}) custom-call(bf16[128,1024]{1,0:T(8,128)(2,1)S(1)} %bitcast.36, bf16[128,1024]{1,0:T(8,128)(2,1)S(1)} %bitcast.37, bf16[128,2048]{1,0:T(8,128)(2,1)S(1)} %bitcast.33, bf16[128,2048]{1,0:T(8,128)(2,1)S(1)} %bitcast.34, ...), custom_call_target="tpu_custom_call" | custom-call | flops 20000000000 | bytes 2000000 | tf_op jit(solution)/shard_map/mixer/pallas_call | solution.py:304
  79.3 0.0 copy-start.10
  79.3 0.8 copy-done.10
  80.1 0.6 copy-done.11
  80.8 180.7 %moe.1 = f32[128,2048]{1,0:T(8,128)} custom-call(bf16[128,2048]{1,0:T(8,128)(2,1)} %copy-done.10, f32[8,24,128]{2,1,0:T(8,128)} %copy-done.11, bf16[2048,512]{1,0:T(8,128)(2,1)} %bitcast.41, bf16[2048,512]{1,0:T(8,128)(2,1)} %bitcast.42, bf16[512,2048]{1,0:T(8,128)(2,1)} %bitcast.43), custom_call_target="tpu_custom_call" | custom-call | flops 12000000000 | bytes 10000000 | tf_op jit(solution)/shard_map/moe/pallas_call | solution.py:575
  261.5 0.6 multiply_reduce_fusion.1
  262.8 1.4 multiply_reduce_fusion
  264.2 0.9 fusion
  (18 shorter events, 0.0 us)
Async XLA Ops:
  3.1 0.7 copy-start
  3.8 0.7 copy-start.1
  4.5 1.2 copy-start.2
  5.8 1.0 copy-start.3
  6.8 1.0 copy-start.4
  7.8 1.0 copy-start.5
  8.9 0.9 copy-start.6
  9.8 0.9 copy-start.7
  10.8 0.7 copy-start.8
  11.5 0.7 copy-start.9
  79.3 0.8 copy-start.10
  80.1 0.7 copy-start.11
  80.8 180.7 %copy-start.12 = (f32[2048]{0:T(1024)S(1)}, f32[2048]{0:T(1024)}, u32[]{:S(2)}) copy-start(f32[2048]{0:T(1024)} %param.33) | copy-start | bytes 24580
  261.5 2.8 %copy-start.13 = (s32[1,128]{1,0:T(1,128)S(1)}, s32[1,128]{1,0:T(1,128)}, u32[]{:S(2)}) copy-start(s32[1,128]{1,0:T(1,128)} %param.32) | copy-start | bytes 1540

commit v4 on v3

--- a/solution.py
+++ b/solution.py
@@ -14,7 +14,7 @@
 TOP = 10
 CAP = 4
 N_CTX = 8
-STATE = jnp.float32
+STATE = jnp.bfloat16
 F32 = jnp.float32
 BF16 = jnp.bfloat16
 HIGHEST = lax.Precision.HIGHEST
@@ -47,8 +47,9 @@
 
 
 def mixer_kernel(
-    q_ref, k_ref, v_ref, gate_ref, w_ref, wt_ref, d_ref, dt_ref, gain_ref,
-    res_ref, proj_ref, norm_ref, info_ref, hidden_ref, x_ref, infos_ref,
+    q_hbm, k_hbm, v_hbm, gate_hbm, w_ref, wt_ref, d_ref, dt_ref, gain_ref,
+    res_hbm, proj_hbm, norm_ref, info_ref, hidden_ref, x_ref, infos_ref,
+    q_ref, k_ref, v_ref, gate_ref, res_ref, proj_ref, load_sem,
     lc_ref, lr_ref, loc_ref, qeff_ref, car_ref, off_ref, got_ref, sent_ref, out_ref, wo, infos,
     send_sem, recv_sem, wo_send, wo_recv, info_send, info_recv,
 ):
@@ -57,6 +58,15 @@
     yy, zz = exp // 8, exp % 8
     last = N_CTX - 1
     barrier = pltpu.get_barrier_semaphore()
+    loads = [
+        pltpu.make_async_copy(source, target, load_sem.at[i])
+        for i, (source, target) in enumerate((
+            (q_hbm, q_ref), (k_hbm, k_ref), (v_hbm, v_ref), (gate_hbm, gate_ref),
+            (res_hbm, res_ref), (proj_hbm, proj_ref),
+        ))
+    ]
+    for i in (5, 0, 1, 2, 3, 4):
+        loads[i].start()
 
     def column_peer(k):
         return {"ctx": me, "exp": yy * 8 + (zz + k) % 8}
@@ -77,21 +87,26 @@
     for k in range(1, 8):
         pl.semaphore_signal(barrier, inc=1, device_id=column_peer(k), device_id_type=MESH)
 
-    left, right, opposite = (me + 6) % 8, (me + 2) % 8, (me + 4) % 8
-    partner = {"ctx": me + 1 - 2 * (me % 2), "exp": exp}
+    core = me % 2
+    side = 1 - 2 * core
+    other = me + side
+    partner = {"ctx": other, "exp": exp}
+    onward = chain_peer(2 * side)
+    near, near_other = (me - 2 * side + 8) % 8, (other - 2 * side + 8) % 8
+    far, far_other = (me + 4) % 8, (other + 4) % 8
     routes = (
-        (None, me, 0, chain_peer(2)), (None, me, 1, chain_peer(2)),
-        (None, me, 0, chain_peer(-2)), (None, me, 1, chain_peer(-2)),
         (None, me, 0, partner), (None, me, 1, partner),
-        (left, left, 0, chain_peer(2)), (right, right, 1, chain_peer(-2)),
-        (left, left, 0, partner), (left, left, 1, partner),
-        (right, right, 0, partner), (right, right, 1, partner),
-        (opposite, opposite, 0, partner), (opposite, opposite, 1, partner),
+        (None, me, 0, onward), (None, me, 1, onward),
+        (other, other, 0, onward), (other, other, 1, onward),
+        (near, near, core, onward), (near_other, near_other, core, onward),
+        (near, near, 0, partner), (near, near, 1, partner),
+        (near_other, near_other, 0, partner), (near_other, near_other, 1, partner),
+        (far, far, core, partner), (far_other, far_other, core, partner),
     )
 
     def shard(n):
         held, index, h, device = routes[n]
-        at = pl.ds(h * 128, 128)
+        at = pl.ds(pl.multiple_of(h * 128, 128), 128)
         return pltpu.make_async_remote_copy(
             src_ref=proj_ref.at[at] if held is None else wo.at[held, at],
             dst_ref=wo.at[index, at],
@@ -128,16 +143,26 @@
             device_id=column_peer(k),
             device_id_type=MESH,
         ).start()
-    for n in (0, 3, 1, 2, 4, 5):
+    loads[5].wait()
+    for n in (2, 3, 0, 1):
         shard(n).start()
     infos[zz] = info_ref[...]
     wo[me] = proj_ref[...]
+    for i in (0, 1, 2):
+        loads[i].wait()
     in_16 = (rows // 16 == cols // 16) & (rows > cols)
 
     def column(array, h):
         return jnp.sum(jnp.where(head_lane == h, array, 0.0), axis=1, keepdims=True)
 
     def maps(step, carry):
+        @pl.when(step == 1)
+        def _():
+            for n in (0, 1):
+                shard(n).wait_recv()
+            for n in (4, 5):
+                shard(n).start()
+
         groups = [step * 2, step * 2 + 1]
         per_group = []
         for g in groups:
@@ -201,10 +226,16 @@
 
     lax.fori_loop(0, KH // 2, maps, 0)
 
-    shard(0).wait_recv()
-    shard(6).start()
-    shard(3).wait_recv()
-    shard(7).start()
+    def relieve():
+        for n in (4, 5):
+            shard(n).wait_recv()
+        for n in (7, 10, 11):
+            shard(n).start()
+
+    for n in (2, 3):
+        shard(n).wait_recv()
+    for n in (6, 8, 9):
+        shard(n).start()
 
     def hop(h):
         return pltpu.make_async_remote_copy(
@@ -232,6 +263,10 @@
     @pl.when((me > 0) & (me < last))
     def _():
         def relay(h, carry):
+            @pl.when(h == 8)
+            def _():
+                relieve()
+
             hop(h).wait_recv()
             s = got_ref[h].astype(F32)
             sent_ref[h] = (fraction(h) * s + off_ref[h] - mm(car_ref[h], s, 2, 2)).astype(STATE)
@@ -240,12 +275,12 @@
 
         lax.fori_loop(0, HEADS, relay, 0)
 
-    shard(8).start()
-    shard(11).start()
-    for n in (1, 2):
-        shard(n).wait_recv()
-    shard(9).start()
-    shard(10).start()
+    @pl.when((me == 0) | (me == last))
+    def _():
+        relieve()
+
+    loads[3].wait()
+    loads[4].wait()
 
     gain = gain_ref[...]
 
@@ -266,7 +301,7 @@
     for n in (6, 7):
         shard(n).wait_recv()
         shard(n + 6).start()
-    for n in (4, 5, 8, 9, 10, 11, 12, 13):
+    for n in (8, 9, 10, 11, 12, 13):
         shard(n).wait_recv()
 
     def project(i, total):
@@ -308,9 +343,19 @@
             jax.ShapeDtypeStruct((T, D), BF16),
             jax.ShapeDtypeStruct((8, 24, T), F32),
         ],
-        in_specs=[pl.BlockSpec(memory_space=pltpu.VMEM)] * 13,
+        in_specs=[
+            pl.BlockSpec(memory_space=pl.ANY if i in (0, 1, 2, 3, 9, 10) else pltpu.VMEM)
+            for i in range(13)
+        ],
         out_specs=[pl.BlockSpec(memory_space=pltpu.VMEM)] * 3,
         scratch_shapes=[
+            pltpu.VMEM((T, KH * DK), BF16),
+            pltpu.VMEM((T, KH * DK), BF16),
+            pltpu.VMEM((T, HEADS * DV), BF16),
+            pltpu.VMEM((T, HEADS * DV), BF16),
+            pltpu.VMEM((T, D), BF16),
+            pltpu.VMEM((256, D), BF16),
+            pltpu.SemaphoreType.DMA((6,)),
             pltpu.VMEM((T, HEADS), F32),
             pltpu.VMEM((HEADS, T), F32),
             square, square, square, square,
@@ -327,7 +372,7 @@
             pltpu.SemaphoreType.DMA,
         ],
         compiler_params=pltpu.CompilerParams(
-            collective_id=0, has_side_effects=True, vmem_limit_bytes=40 * 2**20
+            collective_id=0, has_side_effects=True, vmem_limit_bytes=62 * 2**20
         ),
         cost_estimate=pl.CostEstimate(flops=20 * 10**9, bytes_accessed=2 * 10**6, transcendentals=0),
         name="mixer",
@@ -345,6 +390,7 @@
     ((1, 0), (1, 1), (2, 0), (2, 1), (3, 0), (3, 1), (4, 0)),
     ((1, 1), (1, 0), (2, 1), (2, 0), (3, 1), (3, 0), (4, 1)),
 )
+WIDE = D // 2
 RS_CHUNKS = (
     ((4, 1), (3, 0), (3, 1), (2, 0), (2, 1), (1, 0), (1, 1)),
     ((4, 0), (3, 1), (3, 0), (2, 1), (2, 0), (1, 1), (1, 0)),
@@ -356,7 +402,7 @@
 
 def moe_kernel(
     x_ref, info_ref, wg_hbm, wu_hbm, wd_hbm, out_ref,
-    xg, stage, rows, outb, ret, rs_out, rs_in, y_ref, pick, high, low, wg, wu, wd,
+    act_ref, xg, stage, rows, outb, ret, rs_out, rs_in, y_ref, pick, high, low, wg, wu, wd,
     w_sem, ag_send, ag_recv, in_send, in_recv, back_send, back_recv, rs_send, rs_recv,
 ):
     ctx = lax.axis_index("ctx")
@@ -450,35 +496,38 @@
             high[g, at, :] = top
             low[g, at, :] = (scaled - top.astype(F32)).astype(BF16)
 
-    def tiles(body):
+    def tiles(body, first=0, end=D // 512):
         def run(i, carry):
             body(pl.ds(pl.multiple_of(i * 512, 512), 512))
             return carry
 
-        lax.fori_loop(0, D // 512, run, 0)
+        lax.fori_loop(first, end, run, 0)
+
+    def wide(c):
+        return pl.ds(c * WIDE, WIDE)
 
     def own(p):
         return pl.ds(pl.multiple_of(p * ROWS, ROWS), ROWS)
 
-    def exchange(src, dst, send, recv, g):
+    def exchange(src, dst, send, recv, g, cols):
         def go(k, carry):
             p, device = peer(k)
             pltpu.make_async_remote_copy(
-                src_ref=src.at[g, own(p)],
-                dst_ref=dst.at[g, own(mine)],
-                send_sem=send.at[g],
-                recv_sem=recv.at[g],
+                src_ref=src.at[g, own(p), cols],
+                dst_ref=dst.at[g, own(mine), cols],
+                send_sem=send,
+                recv_sem=recv,
                 device_id=device,
                 device_id_type=MESH,
             ).start()
             return carry
 
         lax.fori_loop(1, PEERS, go, 0)
-        dst[g, own(mine)] = src[g, own(mine)]
-
-    def all_of(ref, sem, g):
-        some = ref.at[g, pl.ds(0, GROUP - ROWS)]
-        return pltpu.make_async_copy(some, some, sem.at[g])
+        dst[g, own(mine), cols] = src[g, own(mine), cols]
+
+    def all_of(ref, sem, g, cols):
+        some = ref.at[g, pl.ds(0, GROUP - ROWS), cols]
+        return pltpu.make_async_copy(some, some, sem)
 
     def dispatch(g):
         def tile(at):
@@ -486,25 +535,31 @@
             stage[g, :, at] = jnp.dot(pick[g], x, preferred_element_type=F32).astype(BF16)
 
         tiles(tile)
-        exchange(stage, rows, in_send, in_recv, g)
+        exchange(stage, rows, in_send.at[g], in_recv.at[g], g, pl.ds(0, D))
 
     def experts(g):
-        all_of(rows, in_recv, g).wait()
+        all_of(rows, in_recv.at[g], g, pl.ds(0, D)).wait()
 
         def tile(i, carry):
             at = pl.ds(pl.multiple_of(i * 256, 256), 256)
             x = rows[g, at, :]
             gate = jnp.dot(x, wg[...], preferred_element_type=F32)
             up = jnp.dot(x, wu[...], preferred_element_type=F32)
-            act = (gate / (1.0 + jnp.exp(-gate)) * up).astype(BF16)
-            outb[g, at, :] = jnp.dot(act, wd[...], preferred_element_type=F32).astype(BF16)
+            act_ref[at, :] = (gate / (1.0 + jnp.exp(-gate)) * up).astype(BF16)
             return carry
 
         lax.fori_loop(0, GROUP // 256, tile, 0)
-        exchange(outb, ret, back_send, back_recv, g)
-
-    def combine(g):
-        all_of(ret, back_recv, g).wait()
+        for c in (0, 1):
+            def down(at):
+                outb[g, :, at] = jnp.dot(
+                    act_ref[...], wd[:, at], preferred_element_type=F32
+                ).astype(BF16)
+
+            tiles(down, 2 * c, 2 * c + 2)
+            exchange(outb, ret, back_send.at[g, c], back_recv.at[g, c], g, wide(c))
+
+    def combine(g, c):
+        all_of(ret, back_recv.at[g, c], g, wide(c)).wait()
 
         def tile(at):
             r = ret[g, :, at]
@@ -513,7 +568,7 @@
             )
             y_ref[g * 4 : g * 4 + 4, :, at] = total.reshape(4, T, 512)
 
-        tiles(tile)
+        tiles(tile, 2 * c, 2 * c + 2)
 
     tables(0)
     pass_on(0, 2)
@@ -526,44 +581,60 @@
         copy.wait()
     experts(0)
     experts(1)
-    combine(0)
-    combine(1)
-
-    def reduce(way, i):
+
+    def reduce(c, way, i):
         return pltpu.make_async_remote_copy(
-            src_ref=rs_out.at[way, i],
-            dst_ref=rs_in.at[way, i],
-            send_sem=rs_send.at[way, i],
-            recv_sem=rs_recv.at[way, i],
+            src_ref=rs_out.at[way, i, :, wide(c)],
+            dst_ref=rs_in.at[way, i, :, wide(c)],
+            send_sem=rs_send.at[c, way, i],
+            recv_sem=rs_recv.at[c, way, i],
             device_id=along((1, -1)[way]),
             device_id_type=MESH,
         )
 
-    for i in range(7):
+    def reduce_step(c, i):
         for way in (0, 1):
             d, h = RS_CHUNKS[way][i]
-            part = y_ref[(AHEAD, BEHIND)[way][d], half(h)]
+            part = y_ref[(AHEAD, BEHIND)[way][d], half(h), wide(c)]
             if i >= 2:
-                reduce(way, i - 2).wait_recv()
-                part = part + rs_in[way, i - 2].astype(F32)
-            rs_out[way, i] = part.astype(BF16)
-            reduce(way, i).start()
-    for i in (5, 6):
-        for way in (0, 1):
-            reduce(way, i).wait_recv()
-    for h in (0, 1):
-        total = y_ref[0, half(h)]
-        for way in (0, 1):
-            total = total + rs_in[way, RS_CHUNKS[way].index((1, h))].astype(F32)
-        out_ref[half(h)] = total
+                reduce(c, way, i - 2).wait_recv()
+                part = part + rs_in[way, i - 2, :, wide(c)].astype(F32)
+            rs_out[way, i, :, wide(c)] = part.astype(BF16)
+            reduce(c, way, i).start()
+
+    combine(1, 0)
+    reduce_step(0, 0)
+    reduce_step(0, 1)
+    combine(0, 0)
+    for i in range(2, 5):
+        reduce_step(0, i)
+    combine(1, 1)
+    reduce_step(1, 0)
+    reduce_step(0, 5)
+    reduce_step(1, 1)
+    reduce_step(0, 6)
+    combine(0, 1)
+    for i in range(2, 7):
+        reduce_step(1, i)
+    for c in (0, 1):
+        for i in (5, 6):
+            for way in (0, 1):
+                reduce(c, way, i).wait_recv()
+        for h in (0, 1):
+            total = y_ref[0, half(h), wide(c)]
+            for way in (0, 1):
+                total = total + rs_in[way, RS_CHUNKS[way].index((1, h)), :, wide(c)].astype(F32)
+            out_ref[half(h), wide(c)] = total
 
     for i in range(7):
         for way in (0, 1):
             gather(way, i).wait_send()
-            reduce(way, i).wait_send()
+            for c in (0, 1):
+                reduce(c, way, i).wait_send()
     for g in (0, 1):
-        all_of(stage, in_send, g).wait()
-        all_of(outb, back_send, g).wait()
+        all_of(stage, in_send.at[g], g, pl.ds(0, D)).wait()
+        for c in (0, 1):
+            all_of(outb, back_send.at[g, c], g, wide(c)).wait()
 
 
 def moe(x, info, w_gate, w_up, w_down):
@@ -578,13 +649,14 @@
         in_specs=[vmem, vmem, anywhere, anywhere, anywhere],
         out_specs=vmem,
         scratch_shapes=[
+            pltpu.VMEM((GROUP, 512), BF16),
             pltpu.VMEM((8, T, D), BF16),
             group, group, group, group, ring, ring,
             pltpu.VMEM((8, T, D), F32),
             table, table, table,
             pltpu.VMEM((D, 512), BF16), pltpu.VMEM((D, 512), BF16), pltpu.VMEM((512, D), BF16),
-            dma((3,)), dma((2, 7)), dma((2, 7)), dma((2,)), dma((2,)), dma((2,)), dma((2,)),
-            dma((2, 7)), dma((2, 7)),
+            dma((3,)), dma((2, 7)), dma((2, 7)), dma((2,)), dma((2,)), dma((2, 2)), dma((2, 2)),
+            dma((2, 2, 7)), dma((2, 2, 7)),
         ],
         compiler_params=pltpu.CompilerParams(
             collective_id=1, has_side_effects=True, vmem_limit_bytes=62 * 2**20

time: 266 us -> 234 us (0.88)
  Pallas kernels: 248 us -> 225 us
  local copies, waits for them, and re-layouts: 12.8 us -> 3.62 us
    pallas_call x1, Pallas kernels: 181 us -> 166 us  [moe(): pl.pallas_call(moe_kernel, out_shape=jax.ShapeDtypeStruct((T, D), F32), i...]
    unnamed x29 -> x7, local copies, waits for them, and re-layouts: 11.1 us -> 0.71 us
    pallas_call x1, Pallas kernels: 67.2 us -> 58.3 us  [mixer(): pl.pallas_call(mixer_kernel, out_shape=[jax.ShapeDtypeStruct((T, D), F32)...]
where the time goes in v4:
time: 234 us; the launch traced here: 233 us
  Pallas kernels  225 us (96%)
  other arithmetic  4.37 us (2%)
  local copies, waits for them, and re-layouts  3.62 us (2%)
    pallas_call x1, Pallas kernels, moe(): pl.pallas_call(moe_kernel, out_shape=jax.ShapeDtypeStruct((T, D), F32), i...  166 us
    pallas_call x1, Pallas kernels, mixer(): pl.pallas_call(mixer_kernel, out_shape=[jax.ShapeDtypeStruct((T, D), F32)...  58.3 us

profile of v4, /device:TPU:5, one launch (start us, length us, event | category | flops | bytes accessed | tf_op | source)
XLA Modules:
  0.0 233.4 jit_solution(5147878613971776417)
XLA Ops:
  0.0 1.4 copy.19.w_ref
  1.4 1.4 copy.20.d_ref
  2.8 0.7 copy.26
  3.5 0.7 fusion.1
  4.2 0.1 pad.2.clone
  4.3 0.7 maximum_maximum_fusion.info_ref
  5.0 58.3 %mixer.1 = (f32[128,2048]{1,0:T(8,128)}, bf16[128,2048]{1,0:T(8,128)(2,1)}, f32[8,24,128]{2,1,0:T(8,128)}) custom-call(bf16[128,1024]{1,0:T(8,128)(2,1)} %bitcast.40, bf16[128,1024]{1,0:T(8,128)(2,1)} %bitcast.41, bf16[128,2048]{1,0:T(8,128)(2,1)} %bitcast.37, bf16[128,2048]{1,0:T(8,128)(2,1)} %bitcast.38, f32[128,16]{1,0:T(8,128)} %copy.19.w_ref, ...), custom_call_target="tpu_custom_call" | custom-call | flops 20000000000 | bytes 2000000 | tf_op jit(solution)/shard_map/mixer/pallas_call | solution.py:339
  63.3 0.0 copy-start.1
  63.3 0.0 copy-start
  63.3 166.4 %moe.1 = f32[128,2048]{1,0:T(8,128)} custom-call(bf16[128,2048]{1,0:T(8,128)(2,1)} %get-tuple-element.9.x_ref, f32[8,24,128]{2,1,0:T(8,128)} %get-tuple-element.10.info_ref, bf16[2048,512]{1,0:T(8,128)(2,1)} %bitcast.34, bf16[2048,512]{1,0:T(8,128)(2,1)} %bitcast.35, bf16[512,2048]{1,0:T(8,128)(2,1)} %bitcast.36), custom_call_target="tpu_custom_call" | custom-call | flops 12000000000 | bytes 10000000 | tf_op jit(solution)/shard_map/moe/pallas_call | solution.py:646
  229.7 0.0 copy-start.2
  229.7 0.0 copy-done.1
  229.7 0.6 multiply_reduce_fusion.1
  231.0 0.0 copy-done
  231.0 1.4 multiply_reduce_fusion
  232.5 0.0 copy-done.2
  232.5 0.9 fusion
  (3 shorter events, 0.0 us)
Async XLA Ops:
  63.3 166.4 %copy-start.1 = (f32[2048]{0:T(1024)S(1)}, f32[2048]{0:T(1024)}, u32[]{:S(2)}) copy-start(f32[2048]{0:T(1024)} %param.33) | copy-start | bytes 24580
  63.3 167.8 %copy-start = (f32[128,2048]{1,0:T(8,128)S(1)}, f32[128,2048]{1,0:T(8,128)}, u32[]{:S(2)}) copy-start(f32[128,2048]{1,0:T(8,128)} %get-tuple-element.8) | copy-start | bytes 3145732
  229.7 2.8 %copy-start.2 = (s32[1,128]{1,0:T(1,128)S(1)}, s32[1,128]{1,0:T(1,128)}, u32[]{:S(2)}) copy-start(s32[1,128]{1,0:T(1,128)} %param.32) | copy-start | bytes 1540

commit v5 on v4

--- a/solution.py
+++ b/solution.py
@@ -47,10 +47,10 @@
 
 
 def mixer_kernel(
-    q_hbm, k_hbm, v_hbm, gate_hbm, w_ref, wt_ref, d_ref, dt_ref, gain_ref,
+    q_hbm, k_hbm, v_hbm, gate_hbm, wt_ref, dt_ref, gain_ref,
     res_hbm, proj_hbm, norm_ref, info_ref, hidden_ref, x_ref, infos_ref,
     q_ref, k_ref, v_ref, gate_ref, res_ref, proj_ref, load_sem,
-    lc_ref, lr_ref, loc_ref, qeff_ref, car_ref, off_ref, got_ref, sent_ref, out_ref, wo, infos,
+    lc_ref, wc_ref, lr_ref, loc_ref, qeff_ref, car_ref, off_ref, got_ref, sent_ref, out_ref, wo, infos,
     send_sem, recv_sem, wo_send, wo_recv, info_send, info_recv,
 ):
     me = lax.axis_index("ctx")
@@ -94,19 +94,37 @@
     onward = chain_peer(2 * side)
     near, near_other = (me - 2 * side + 8) % 8, (other - 2 * side + 8) % 8
     far, far_other = (me + 4) % 8, (other + 4) % 8
+    y_mate = {"ctx": me, "exp": (yy + 1 - 2 * (yy % 2)) * 8 + zz}
+    z_mate = {"ctx": me, "exp": yy * 8 + zz + 1 - 2 * (zz % 2)}
+    far_mate = {
+        "ctx": me,
+        "exp": (yy + (1 - core) * (1 - 2 * (yy % 2))) * 8 + zz + core * (1 - 2 * (zz % 2)),
+    }
+    pl.semaphore_signal(barrier, inc=1, device_id=y_mate, device_id_type=MESH)
+    first, second = (yy % 2) * 64, 128 + (zz % 2) * 64
+    first_rest, second_rest = 64 - first, 128 + 64 - (zz % 2) * 64
+    fetched = first + core * (second - first)
+    rest = first_rest + core * (second_rest - first_rest)
     routes = (
-        (None, me, 0, partner), (None, me, 1, partner),
-        (None, me, 0, onward), (None, me, 1, onward),
-        (other, other, 0, onward), (other, other, 1, onward),
-        (near, near, core, onward), (near_other, near_other, core, onward),
-        (near, near, 0, partner), (near, near, 1, partner),
-        (near_other, near_other, 0, partner), (near_other, near_other, 1, partner),
-        (far, far, core, partner), (far_other, far_other, core, partner),
+        (None, me, 0, 128, partner), (None, me, 128, 128, partner),
+        (None, me, first, 64, onward), (None, me, second, 64, onward),
+        (other, other, first, 64, onward), (other, other, second, 64, onward),
+        (near, near, fetched, 64, onward), (near_other, near_other, fetched, 64, onward),
+        (near, near, first, 64, partner), (near, near, second, 64, partner),
+        (near_other, near_other, first, 64, partner), (near_other, near_other, second, 64, partner),
+        (far, far, fetched, 64, partner), (far_other, far_other, fetched, 64, partner),
+        (near, near, first, 64, y_mate), (near, near, second, 64, z_mate),
+        (near_other, near_other, first, 64, y_mate), (near_other, near_other, second, 64, z_mate),
+        (far, far, fetched, 64, far_mate), (far_other, far_other, fetched, 64, far_mate),
+        (near, near, first_rest, 64, partner), (near, near, second_rest, 64, partner),
+        (near_other, near_other, first_rest, 64, partner),
+        (near_other, near_other, second_rest, 64, partner),
+        (far, far, rest, 64, partner), (far_other, far_other, rest, 64, partner),
     )
 
     def shard(n):
-        held, index, h, device = routes[n]
-        at = pl.ds(pl.multiple_of(h * 128, 128), 128)
+        held, index, start, size, device = routes[n]
+        at = pl.ds(pl.multiple_of(start, 64), size)
         return pltpu.make_async_remote_copy(
             src_ref=proj_ref.at[at] if held is None else wo.at[held, at],
             dst_ref=wo.at[index, at],
@@ -116,23 +134,37 @@
             device_id_type=MESH,
         )
 
+    def take(*numbers):
+        for n in numbers:
+            shard(n).wait_recv()
+
+    def give(*numbers):
+        for n in numbers:
+            shard(n).start()
+
     rows = lax.broadcasted_iota(jnp.int32, (T, T), 0)
     cols = lax.broadcasted_iota(jnp.int32, (T, T), 1)
     lower = (rows >= cols).astype(F32)
     upper = (rows <= cols).astype(F32)
     eye = (rows == cols).astype(F32)
-    lc_ref[...] = jnp.dot(lower, jnp.log(d_ref[...]), precision=HIGHEST, preferred_element_type=F32)
+    by_row = (((1,), (1,)), ((), ()))
+    lc_ref[...] = lax.dot_general(
+        lower, jnp.log(dt_ref[...]), by_row, precision=HIGHEST, preferred_element_type=F32
+    )
+    wc_ref[...] = lax.dot_general(
+        eye, wt_ref[...], by_row, precision=HIGHEST, preferred_element_type=F32
+    )
     lr_ref[...] = jnp.dot(jnp.log(dt_ref[...]), upper, precision=HIGHEST, preferred_element_type=F32)
     ones = jnp.ones((8, DK), F32)
     head_lane = lax.broadcasted_iota(jnp.int32, (T, HEADS), 1)
 
     @pl.when((me > 0) & (me < last))
     def _():
-        pl.semaphore_wait(barrier, 11)
+        pl.semaphore_wait(barrier, 12)
 
     @pl.when((me == 0) | (me == last))
     def _():
-        pl.semaphore_wait(barrier, 10)
+        pl.semaphore_wait(barrier, 11)
 
     for k in range(1, 8):
         pltpu.make_async_remote_copy(
@@ -144,8 +176,7 @@
             device_id_type=MESH,
         ).start()
     loads[5].wait()
-    for n in (2, 3, 0, 1):
-        shard(n).start()
+    give(2, 3, 0, 1)
     infos[zz] = info_ref[...]
     wo[me] = proj_ref[...]
     for i in (0, 1, 2):
@@ -158,10 +189,13 @@
     def maps(step, carry):
         @pl.when(step == 1)
         def _():
-            for n in (0, 1):
-                shard(n).wait_recv()
-            for n in (4, 5):
-                shard(n).start()
+            take(0, 1)
+            give(4, 5)
+
+        @pl.when(step == 3)
+        def _():
+            take(2, 3)
+            give(6, 14, 15, 8, 9)
 
         groups = [step * 2, step * 2 + 1]
         per_group = []
@@ -188,7 +222,7 @@
         state = []
         for (kraw, qu, rk_row, kk, qk, kt), h in heads:
             lcol = column(lc_ref[...], h)
-            wcol = column(w_ref[...], h)
+            wcol = column(wc_ref[...], h)
             lrow = lr_ref[pl.ds(h, 1), :]
             wrow = wt_ref[pl.ds(h, 1), :]
             ratio = jnp.exp(jnp.minimum(lcol - lrow, 0.0)) * lower
@@ -226,16 +260,14 @@
 
     lax.fori_loop(0, KH // 2, maps, 0)
 
+    take(4, 5)
+    give(7, 16, 17, 10, 11)
+
     def relieve():
-        for n in (4, 5):
-            shard(n).wait_recv()
-        for n in (7, 10, 11):
-            shard(n).start()
-
-    for n in (2, 3):
-        shard(n).wait_recv()
-    for n in (6, 8, 9):
-        shard(n).start()
+        take(6, 7)
+        give(18, 19, 12, 13)
+        take(14, 15, 16, 17)
+        give(20, 21, 22, 23)
 
     def hop(h):
         return pltpu.make_async_remote_copy(
@@ -263,7 +295,7 @@
     @pl.when((me > 0) & (me < last))
     def _():
         def relay(h, carry):
-            @pl.when(h == 8)
+            @pl.when(h == 10)
             def _():
                 relieve()
 
@@ -298,11 +330,9 @@
 
     lax.fori_loop(0, HEADS, finish, 0)
 
-    for n in (6, 7):
-        shard(n).wait_recv()
-        shard(n + 6).start()
-    for n in (8, 9, 10, 11, 12, 13):
-        shard(n).wait_recv()
+    take(18, 19)
+    give(24, 25)
+    take(*range(8, 14), *range(20, 26))
 
     def project(i, total):
         at = pl.ds(pl.multiple_of(i * 512, 512), 512)
@@ -320,7 +350,7 @@
     pltpu.make_async_copy(seven, seven, info_recv).wait()
     pltpu.make_async_copy(seven, seven, info_send).wait()
     infos_ref[...] = infos[...]
-    for n in range(14):
+    for n in range(26):
         shard(n).wait_send()
 
     @pl.when(me < last)
@@ -344,8 +374,8 @@
             jax.ShapeDtypeStruct((8, 24, T), F32),
         ],
         in_specs=[
-            pl.BlockSpec(memory_space=pl.ANY if i in (0, 1, 2, 3, 9, 10) else pltpu.VMEM)
-            for i in range(13)
+            pl.BlockSpec(memory_space=pl.ANY if i in (0, 1, 2, 3, 7, 8) else pltpu.VMEM)
+            for i in range(11)
         ],
         out_specs=[pl.BlockSpec(memory_space=pltpu.VMEM)] * 3,
         scratch_shapes=[
@@ -357,6 +387,7 @@
             pltpu.VMEM((256, D), BF16),
             pltpu.SemaphoreType.DMA((6,)),
             pltpu.VMEM((T, HEADS), F32),
+            pltpu.VMEM((T, HEADS), F32),
             pltpu.VMEM((HEADS, T), F32),
             square, square, square, square,
             pltpu.VMEM((HEADS, DK, DV), STATE),
@@ -366,8 +397,8 @@
             pltpu.VMEM((8, 24, T), F32),
             pltpu.SemaphoreType.DMA((HEADS,)),
             pltpu.SemaphoreType.DMA((HEADS,)),
-            pltpu.SemaphoreType.DMA((14,)),
-            pltpu.SemaphoreType.DMA((14,)),
+            pltpu.SemaphoreType.DMA((26,)),
+            pltpu.SemaphoreType.DMA((26,)),
             pltpu.SemaphoreType.DMA,
             pltpu.SemaphoreType.DMA,
         ],
@@ -377,7 +408,7 @@
         cost_estimate=pl.CostEstimate(flops=20 * 10**9, bytes_accessed=2 * 10**6, transcendentals=0),
         name="mixer",
     )(
-        queries, keys, values, out_gate, write_rate, write_rate.T, decay, decay.T, head_gain[None, :],
+        queries, keys, values, out_gate, write_rate.T, decay.T, head_gain[None, :],
         residual, out_proj, ffn_gain[None, :], listed,
     )
 

time: 234 us -> 224 us (0.957)
  Pallas kernels: 225 us -> 218 us
  local copies, waits for them, and re-layouts: 3.62 us -> 0.79 us
    pallas_call x1, Pallas kernels: 58.3 us -> 50.7 us  [mixer(): pl.pallas_call(mixer_kernel, out_shape=[jax.ShapeDtypeStruct((T, D), F32)...]
    squeeze x2 -> x0, local copies, waits for them, and re-layouts: 2.84 us -> none  [the longest x1 1.42 us: local(): write_rate[0]]
where the time goes in v5:
time: 224 us
  Pallas kernels  218 us (97%)
  other arithmetic  4.36 us (2%)
    pallas_call x1, Pallas kernels, moe(): pl.pallas_call(moe_kernel, out_shape=jax.ShapeDtypeStruct((T, D), F32), i...  167 us
    pallas_call x1, Pallas kernels, mixer(): pl.pallas_call(mixer_kernel, out_shape=[jax.ShapeDtypeStruct((T, D), F32)...  50.7 us

profile of v5, /device:TPU:5, one launch (start us, length us, event | category | flops | bytes accessed | tf_op | source)
XLA Modules:
  0.0 224.0 jit_solution(9718006289114389758)
XLA Ops:
  0.0 0.7 copy.24
  0.7 0.7 fusion.1
  1.4 0.1 pad.2.clone
  1.5 0.7 maximum_maximum_fusion.info_ref
  2.1 50.7 %mixer.1 = (f32[128,2048]{1,0:T(8,128)}, bf16[128,2048]{1,0:T(8,128)(2,1)}, f32[8,24,128]{2,1,0:T(8,128)}) custom-call(bf16[128,1024]{1,0:T(8,128)(2,1)} %bitcast.36, bf16[128,1024]{1,0:T(8,128)(2,1)} %bitcast.37, bf16[128,2048]{1,0:T(8,128)(2,1)} %bitcast.33, bf16[128,2048]{1,0:T(8,128)(2,1)} %bitcast.34, f32[16,128]{1,0:T(8,128)} %bitcast.38, ...), custom_call_target="tpu_custom_call" | custom-call | flops 20000000000 | bytes 2000000 | tf_op jit(solution)/shard_map/mixer/pallas_call | solution.py:369
  52.9 0.0 copy-start.1
  52.9 0.0 copy-start
  52.9 167.3 %moe.1 = f32[128,2048]{1,0:T(8,128)} custom-call(bf16[128,2048]{1,0:T(8,128)(2,1)} %get-tuple-element.9.x_ref, f32[8,24,128]{2,1,0:T(8,128)} %get-tuple-element.10.info_ref, bf16[2048,512]{1,0:T(8,128)(2,1)} %bitcast.30, bf16[2048,512]{1,0:T(8,128)(2,1)} %bitcast.31, bf16[512,2048]{1,0:T(8,128)(2,1)} %bitcast.32), custom_call_target="tpu_custom_call" | custom-call | flops 12000000000 | bytes 10000000 | tf_op jit(solution)/shard_map/moe/pallas_call | solution.py:677
  220.3 0.0 copy-start.2
  220.3 0.0 copy-done.1
  220.3 0.6 multiply_reduce_fusion.1
  221.6 0.0 copy-done
  221.6 1.4 multiply_reduce_fusion
  223.0 0.0 copy-done.2
  223.0 0.9 fusion
  (3 shorter events, 0.0 us)
Async XLA Ops:
  52.9 167.4 %copy-start.1 = (f32[2048]{0:T(1024)S(1)}, f32[2048]{0:T(1024)}, u32[]{:S(2)}) copy-start(f32[2048]{0:T(1024)} %param.33) | copy-start | bytes 24580
  52.9 168.7 %copy-start = (f32[128,2048]{1,0:T(8,128)S(1)}, f32[128,2048]{1,0:T(8,128)}, u32[]{:S(2)}) copy-start(f32[128,2048]{1,0:T(8,128)} %get-tuple-element.8) | copy-start | bytes 3145732
  220.3 2.8 %copy-start.2 = (s32[1,128]{1,0:T(1,128)S(1)}, s32[1,128]{1,0:T(1,128)}, u32[]{:S(2)}) copy-start(s32[1,128]{1,0:T(1,128)} %param.32) | copy-start | bytes 1540

commit v6 on v5

--- a/solution.py
+++ b/solution.py
@@ -469,13 +469,17 @@
     def half(h):
         return pl.ds(h * HALF, HALF)
 
+    def wide(c):
+        return pl.ds(c * WIDE, WIDE)
+
     def gather(way, i):
-        d, h = AG_CHUNKS[way][i]
+        d, h = AG_CHUNKS[way][i % 7]
         slot = (BEHIND, AHEAD)[way]
-        src = x_ref.at[half(h)] if d == 1 else xg.at[slot[d - 1], half(h)]
+        cols = wide(i // 7)
+        src = x_ref.at[half(h), cols] if d == 1 else xg.at[slot[d - 1], half(h), cols]
         return pltpu.make_async_remote_copy(
             src_ref=src,
-            dst_ref=xg.at[slot[d], half(h)],
+            dst_ref=xg.at[slot[d], half(h), cols],
             send_sem=ag_send.at[way, i],
             recv_sem=ag_recv.at[way, i],
             device_id=along((1, -1)[way]),
@@ -486,7 +490,7 @@
         for i in range(first, end):
             for way in (0, 1):
                 gather(way, i).wait_recv()
-                if i + 2 < 7:
+                if i + 2 < 14:
                     gather(way, i + 2).start()
 
     for i in (0, 1):
@@ -505,8 +509,8 @@
     ).astype(F32).astype(BF16)
     named = (lax.broadcasted_iota(jnp.int32, (PEERS, T), 0) * 8 + zz).astype(F32)
 
-    def tables(g):
-        for s in range(4):
+    def tables(g, *sources):
+        for s in sources:
             info = info_ref[(zz + OFFSETS[g * 4 + s] + 8) % 8]
             member = jnp.zeros((PEERS, T), F32)
             weight = jnp.zeros((PEERS, T), F32)
@@ -534,9 +538,6 @@
 
         lax.fori_loop(first, end, run, 0)
 
-    def wide(c):
-        return pl.ds(c * WIDE, WIDE)
-
     def own(p):
         return pl.ds(pl.multiple_of(p * ROWS, ROWS), ROWS)
 
@@ -560,16 +561,17 @@
         some = ref.at[g, pl.ds(0, GROUP - ROWS), cols]
         return pltpu.make_async_copy(some, some, sem)
 
-    def dispatch(g):
+    def dispatch(g, c):
         def tile(at):
             x = xg[g * 4 : g * 4 + 4, :, at].reshape(GROUP, 512)
             stage[g, :, at] = jnp.dot(pick[g], x, preferred_element_type=F32).astype(BF16)
 
-        tiles(tile)
-        exchange(stage, rows, in_send.at[g], in_recv.at[g], g, pl.ds(0, D))
+        tiles(tile, 2 * c, 2 * c + 2)
+        exchange(stage, rows, in_send.at[g, c], in_recv.at[g, c], g, wide(c))
 
     def experts(g):
-        all_of(rows, in_recv.at[g], g, pl.ds(0, D)).wait()
+        for c in (0, 1):
+            all_of(rows, in_recv.at[g, c], g, wide(c)).wait()
 
         def tile(i, carry):
             at = pl.ds(pl.multiple_of(i * 256, 256), 256)
@@ -601,13 +603,23 @@
 
         tiles(tile, 2 * c, 2 * c + 2)
 
-    tables(0)
-    pass_on(0, 2)
-    tables(1)
+    tables(0, 0, 1)
+    pass_on(0, 1)
+    tables(0, 2)
+    pass_on(1, 2)
+    tables(0, 3)
     pass_on(2, 4)
-    dispatch(0)
-    pass_on(4, 7)
-    dispatch(1)
+    dispatch(0, 0)
+    pass_on(4, 5)
+    tables(1, 0, 1)
+    pass_on(5, 6)
+    tables(1, 2, 3)
+    pass_on(6, 7)
+    dispatch(1, 0)
+    pass_on(7, 11)
+    dispatch(0, 1)
+    pass_on(11, 14)
+    dispatch(1, 1)
     for copy in weights:
         copy.wait()
     experts(0)
@@ -659,12 +671,12 @@
 
     for i in range(7):
         for way in (0, 1):
-            gather(way, i).wait_send()
             for c in (0, 1):
+                gather(way, i + 7 * c).wait_send()
                 reduce(c, way, i).wait_send()
     for g in (0, 1):
-        all_of(stage, in_send.at[g], g, pl.ds(0, D)).wait()
         for c in (0, 1):
+            all_of(stage, in_send.at[g, c], g, wide(c)).wait()
             all_of(outb, back_send.at[g, c], g, wide(c)).wait()
 
 
@@ -686,7 +698,7 @@
             pltpu.VMEM((8, T, D), F32),
             table, table, table,
             pltpu.VMEM((D, 512), BF16), pltpu.VMEM((D, 512), BF16), pltpu.VMEM((512, D), BF16),
-            dma((3,)), dma((2, 7)), dma((2, 7)), dma((2,)), dma((2,)), dma((2, 2)), dma((2, 2)),
+            dma((3,)), dma((2, 14)), dma((2, 14)), dma((2, 2)), dma((2, 2)), dma((2, 2)), dma((2, 2)),
             dma((2, 2, 7)), dma((2, 2, 7)),
         ],
         compiler_params=pltpu.CompilerParams(

time: 224 us -> 209 us (0.933); the launches traced: 224 us -> 206 us
  Pallas kernels: 218 us -> 200 us
    pallas_call x1, Pallas kernels: 167 us -> 150 us  [moe(): pl.pallas_call(moe_kernel, out_shape=jax.ShapeDtypeStruct((T, D), F32), i...]
where the time goes in v6:
time: 209 us; the launch traced here: 206 us
  Pallas kernels  200 us (96%)
  other arithmetic  4.36 us (2%)
    pallas_call x1, Pallas kernels, moe(): pl.pallas_call(moe_kernel, out_shape=jax.ShapeDtypeStruct((T, D), F32), i...  150 us
    pallas_call x1, Pallas kernels, mixer(): pl.pallas_call(mixer_kernel, out_shape=[jax.ShapeDtypeStruct((T, D), F32)...  50.7 us

profile of v6, /device:TPU:5, one launch (start us, length us, event | category | flops | bytes accessed | tf_op | source)
XLA Modules:
  0.0 206.3 jit_solution(10354273972336965610)
XLA Ops:
  0.0 0.7 copy.24
  0.7 0.7 fusion.1
  1.4 0.1 pad.2.clone
  1.5 0.7 maximum_maximum_fusion.info_ref
  2.1 50.7 %mixer.1 = (f32[128,2048]{1,0:T(8,128)}, bf16[128,2048]{1,0:T(8,128)(2,1)}, f32[8,24,128]{2,1,0:T(8,128)}) custom-call(bf16[128,1024]{1,0:T(8,128)(2,1)} %bitcast.36, bf16[128,1024]{1,0:T(8,128)(2,1)} %bitcast.37, bf16[128,2048]{1,0:T(8,128)(2,1)} %bitcast.33, bf16[128,2048]{1,0:T(8,128)(2,1)} %bitcast.34, f32[16,128]{1,0:T(8,128)} %bitcast.38, ...), custom_call_target="tpu_custom_call" | custom-call | flops 20000000000 | bytes 2000000 | tf_op jit(solution)/shard_map/mixer/pallas_call | solution.py:369
  52.9 0.0 copy-start.1
  52.9 0.0 copy-start
  52.9 149.7 %moe.1 = f32[128,2048]{1,0:T(8,128)} custom-call(bf16[128,2048]{1,0:T(8,128)(2,1)} %get-tuple-element.9.x_ref, f32[8,24,128]{2,1,0:T(8,128)} %get-tuple-element.10.info_ref, bf16[2048,512]{1,0:T(8,128)(2,1)} %bitcast.30, bf16[2048,512]{1,0:T(8,128)(2,1)} %bitcast.31, bf16[512,2048]{1,0:T(8,128)(2,1)} %bitcast.32), custom_call_target="tpu_custom_call" | custom-call | flops 12000000000 | bytes 10000000 | tf_op jit(solution)/shard_map/moe/pallas_call | solution.py:689
  202.6 0.0 copy-start.2
  202.6 0.0 copy-done.1
  202.6 0.6 multiply_reduce_fusion.1
  203.9 0.0 copy-done
  203.9 1.4 multiply_reduce_fusion
  205.4 0.0 copy-done.2
  205.4 0.9 fusion
  (3 shorter events, 0.0 us)
Async XLA Ops:
  52.9 149.7 %copy-start.1 = (f32[2048]{0:T(1024)S(1)}, f32[2048]{0:T(1024)}, u32[]{:S(2)}) copy-start(f32[2048]{0:T(1024)} %param.33) | copy-start | bytes 24580
  52.9 151.0 %copy-start = (f32[128,2048]{1,0:T(8,128)S(1)}, f32[128,2048]{1,0:T(8,128)}, u32[]{:S(2)}) copy-start(f32[128,2048]{1,0:T(8,128)} %get-tuple-element.8) | copy-start | bytes 3145732
  202.6 2.8 %copy-start.2 = (s32[1,128]{1,0:T(1,128)S(1)}, s32[1,128]{1,0:T(1,128)}, u32[]{:S(2)}) copy-start(s32[1,128]{1,0:T(1,128)} %param.32) | copy-start | bytes 1540
